TPU v7x, 512 devices: a whole 4x4x16 slice. The times are simulated.
512 devices in a mesh: member: 16 (over x, z_hi), slab: 32 (over y, z_lo, core).
Axes of the slice: x: 4, y: 4, z: 16 (z_hi: 4, z_lo: 4; z = z_hi * 4 + z_lo), core: 2. Of those that a mesh axis runs over, the one named last changes fastest.
Arguments:
- fluid_head_start: float32 [192, 512, 128], P('member', 'slab'), may hold values from -6 to 6
- conductivity_matrix: float32 [192, 512, 128], P('member', 'slab'), may hold values from 0.1 to 1
- well_rates: float32 [512, 128], P('slab'), may hold values from -3 to 3
- cell_layer: int32 [512, 128], P('slab'), may hold values from 0 to 7
- pixel_coords: int32 [2, 4096], replicated, may hold values from 0 to 63
- obs_index: int32 [1024], replicated, may hold values from 0 to 4095
- obs_value: float32 [1024], replicated, may hold values from -0.6 to 0.6
- obs_sigma: float32 [1024], replicated, may hold values from 0.05 to 0.5
Outputs:
- analysed: float32 [192, 512, 128], P('member', 'slab')
- subsidence: float32 [4096, 192], P(('member', 'slab'))
All inputs are finite; a program needn't handle non-finite values.
Results may differ from a plain program's by a relative error of at most 0.00028.
Values sent between devices are 32-bit elements; how exact they have to be, the bound alone decides.
A program may use at most 64 MiB of HBM per device.

v0:
```python
import math

import jax
import jax.numpy as jnp
from jax import lax
from jax.sharding import PartitionSpec as P

STEPS = 4


time_step = 0.15
pixel_span = 64.0
top_depth = 2.0


def padded(value, sides, width):
    for axis, dim in sides:
        size, length = (lax.axis_size(axis), value.shape[dim])
        up = [(i, (i + 1) % size) for i in range(size - 1)]
        down = [(j, i) for i, j in up]
        last = lax.slice_in_dim(value, length - width, length, axis=dim)
        initial = lax.slice_in_dim(value, 0, width, axis=dim)
        before = lax.ppermute(last, axis, up)
        after = lax.ppermute(initial, axis, down)
        value = jnp.concatenate([before, value, after], axis=dim)
    return value


def advance_in_time(fluid_head_grid, perm_field, source, open_faces):
    mobility = perm_field * (1.0 + 0.5 * jnp.tanh(fluid_head_grid))
    sample_vectors, height, across_cells = fluid_head_grid.shape
    across = 0.5 * (mobility[:, 1:] + mobility[:, :-1]) * open_faces[None, :, None]
    flux_rows = across * (fluid_head_grid[:, 1:] - fluid_head_grid[:, :-1])
    zero_row = jnp.zeros((sample_vectors, 1, across_cells), fluid_head_grid.dtype)
    inflow = jnp.concatenate([flux_rows, zero_row], 1) - jnp.concatenate([zero_row, flux_rows], 1)
    along = 0.5 * (mobility[:, :, 1:] + mobility[:, :, :-1])
    flux_cols = along * (fluid_head_grid[:, :, 1:] - fluid_head_grid[:, :, :-1])
    zero_col = jnp.zeros((sample_vectors, height, 1), fluid_head_grid.dtype)
    inflow = inflow + (
        jnp.concatenate([flux_cols, zero_col], 2) - jnp.concatenate([zero_col, flux_cols], 2)
    )
    return fluid_head_grid + time_step * (inflow + source[None])


def kernel_rows(pixel_x, pixel_y, cell_x, cell_y, depth, volume):
    delta_x = cell_x[None, :] - pixel_x[:, None]
    delta_y = cell_y[None, :] - pixel_y[:, None]
    radius = delta_x * delta_x + delta_y * delta_y + depth[None, :] * depth[None, :]
    return volume * depth[None, :] / (radius * jnp.sqrt(radius))


def gram_terms(predicted, obs_value, obs_sigma, owned):
    centre = jnp.mean(predicted, axis=1)
    anomaly = predicted - centre[:, None]
    inverse_var = 1.0 / (obs_sigma * obs_sigma)
    weighted = anomaly * inverse_var[:, None]
    gram = lax.dot_general(
        anomaly, weighted, (((0,), (0,)), ((), ())), precision=lax.Precision.HIGHEST
    )
    rhs = jnp.dot(owned * (obs_value - centre), weighted, precision=lax.Precision.HIGHEST)
    return (gram, rhs)


def finish(gram, rhs, sample_vector_pile):
    sample_vectors = sample_vector_pile.shape[0]
    ident = jnp.eye(sample_vectors, dtype=gram.dtype)
    gram = gram + (sample_vectors - 1.0) * ident
    factor = jnp.linalg.cholesky(gram)
    inverse = jax.scipy.linalg.solve_triangular(factor, ident, lower=True)
    weights = jnp.dot(
        inverse.T,
        jnp.dot(inverse, rhs, precision=lax.Precision.HIGHEST),
        precision=lax.Precision.HIGHEST,
    )
    transform = jnp.sqrt(sample_vectors - 1.0) * inverse.T
    mix = weights[:, None] + transform
    centre = jnp.mean(sample_vector_pile, axis=0)
    spread = sample_vector_pile - centre[None]
    return centre[None] + lax.dot_general(
        mix, spread, (((0,), (0,)), ((), ())), precision=lax.Precision.HIGHEST
    )


def face_mask(first_global, height, total_rows):
    index = first_global + jnp.arange(height - 1, dtype=jnp.int32)
    return ((index >= 0) & (index + 1 <= total_rows - 1)).astype(jnp.float32)


def shards(
    fluid_head_start,
    conductivity_matrix,
    well_rates,
    cell_layer,
    pixel_coords,
    obs_index,
    obs_value,
    obs_sigma,
):
    local_members, slab_rows, across_cells = fluid_head_start.shape
    member_count = lax.axis_size("member")
    slab_count = lax.axis_size("slab")
    slab_index = lax.axis_index("slab")
    member_index = lax.axis_index("member")
    total_rows = slab_rows * slab_count
    rim_width = STEPS
    static = jnp.concatenate([conductivity_matrix, well_rates[None]], 0)
    static_ext = padded(static, (("slab", 1),), rim_width)
    permeability_extended = static_ext[:-1]
    source_extended = static_ext[-1]
    fluid_head_grid = padded(fluid_head_start, (("slab", 1),), STEPS)
    open_faces = face_mask(slab_index * slab_rows - STEPS, slab_rows + 2 * STEPS, total_rows)
    for repeat in range(STEPS):
        fluid_head_grid = advance_in_time(
            fluid_head_grid, permeability_extended, source_extended, open_faces
        )
    predicted_ensemble = fluid_head_grid[:, STEPS : STEPS + slab_rows]
    collected_states = lax.all_to_all(
        predicted_ensemble, "member", split_axis=1, concat_axis=0, tiled=True
    )
    sample_vectors = collected_states.shape[0]
    sub_rows = collected_states.shape[1]
    sample_vector_pile = collected_states.reshape(sample_vectors, sub_rows * across_cells)
    row_global = (
        slab_index * slab_rows + member_index * sub_rows + jnp.arange(sub_rows, dtype=jnp.int32)
    )
    row_pos = (row_global.astype(jnp.float32) + 0.5) * (pixel_span / total_rows)
    col_pos = (jnp.arange(across_cells).astype(jnp.float32) + 0.5) * (pixel_span / across_cells)
    cell_x = jnp.broadcast_to(row_pos[:, None], (sub_rows, across_cells)).reshape(-1)
    cell_y = col_pos[None, :].reshape(-1)
    layers = lax.dynamic_slice_in_dim(cell_layer, member_index * sub_rows, sub_rows, 0).astype(
        jnp.float32
    )
    depth = (top_depth + layers).reshape(-1)
    volume = pixel_span * pixel_span / (total_rows * across_cells)
    pixel_f = pixel_coords.astype(jnp.float32)
    pixel_total = pixel_coords.shape[1]
    own_rows = pixel_total // (member_count * slab_count)
    own_first = lax.axis_index(("member", "slab")) * own_rows
    block = math.gcd(pixel_total, 512)

    def pixel_block(offset):
        coords = lax.dynamic_slice_in_dim(pixel_f, offset, block, 1)
        kern = kernel_rows(coords[0], coords[1], cell_x, cell_y, depth, volume)
        return lax.dot_general(
            kern, sample_vector_pile, (((1,), (1,)), ((), ())), precision=lax.Precision.HIGHEST
        )

    offsets = 0 + block * jnp.arange(pixel_total // block, dtype=jnp.int32)
    whole = lax.psum(
        lax.map(pixel_block, offsets).reshape(pixel_total, sample_vectors), ("member", "slab")
    )
    own_part = lax.dynamic_slice_in_dim(whole, own_first, own_rows, 0)
    predicted = jnp.take(whole, obs_index, axis=0)
    gram, rhs = gram_terms(predicted, obs_value, obs_sigma, jnp.ones_like(obs_value))
    analysed = finish(gram, rhs, sample_vector_pile).reshape(sample_vectors, sub_rows, across_cells)
    returned = lax.all_to_all(analysed, "member", split_axis=0, concat_axis=1, tiled=True)
    return (returned, own_part)


def solution(mesh):
    return jax.shard_map(
        shards,
        mesh=mesh,
        in_specs=(
            P("member", "slab", None),
            P("member", "slab", None),
            P("slab", None),
            P("slab", None),
            P(),
            P(),
            P(),
            P(),
        ),
        out_specs=(P("member", "slab", None), P(("member", "slab"), None)),
        check_vma=False,
    )
```

profile of v0, /device:TPU:1, one launch (start us, length us, event | category | flops | bytes accessed | tf_op | source)
XLA Modules:
  0.0 676.4 jit_solution(5419804613752783939)
XLA Ops:
  7.2 0.8 fusion.83
  8.0 4.9 collective-permute-start
  13.0 5.1 collective-permute-start.1
  18.1 0.9 copy.28
  19.0 0.7 pad_maximum_fusion.7
  19.7 1.9 collective-permute-start.2
  21.7 2.4 collective-permute-start.3
  24.1 0.9 copy_dynamic-update-slice_fusion
  25.1 2.2 collective-permute-done.3
  27.2 0.7 pad_maximum_fusion.8
  28.0 0.7 pad_maximum_fusion
  28.7 0.2 fusion.40
  29.0 0.1 add_multiply_fusion.3
  29.3 0.2 fusion.38
  29.4 0.1 add_multiply_fusion.2
  29.7 0.2 fusion.36
  29.9 0.1 add_multiply_fusion.1
  30.1 0.2 fusion.34
  30.3 0.8 slice_add_fusion.8
  31.1 14.7 %all-to-all-start = ((f32[12,16,128]{2,0,1:T(8,128)}), f32[12,16,128]{2,0,1:T(8,128)S(1)}, u32[]{:S(2)}, u32[]{:S(2)}) async-start(f32[12,16,128]{2,0,1:T(8,128)} %slice_add_fusion.8), calls=%async_computation | async-start | bytes 262144 | tf_op jit(solution)/shard_map/all_to_all | solution.py:117
  45.9 0.7 fusion.81
  46.6 15.7 %all-to-all-done = f32[12,16,128]{2,0,1:T(8,128)S(1)} async-done(((f32[12,16,128]{2,0,1:T(8,128)}), f32[12,16,128]{2,0,1:T(8,128)S(1)}, u32[]{:S(2)}, u32[]{:S(2)}) %all-to-all-start) | async-done | bytes 98336 | tf_op jit(solution)/shard_map/all_to_all | solution.py:117
  62.3 24.8 %while.14 = (s32[]{:T(128)}, f32[8,512,192]{1,2,0:T(8,128)S(1)}, f32[1,128]{1,0:T(1,128)S(1)}, f32[1,1]{1,0:T(1,128)}, s32[8]{0:T(128)S(1)}, /*index=5*/f32[2,40...) while((s32[]{:T(128)}, f32[8,512,192]{1,2,0:T(8,128)S(1)}, ...), condition=%wide.region_2.3_spmd.clone, body=%wide.region_1.2_spmd.clone.sunk | while | flops 151389696 | bytes 507079 | solution.py:150
  62.3 0.6 dynamic_slice.27
  64.7 0.7 fusion.99
  65.4 0.6 dynamic_slice.27
  67.8 0.7 fusion.99
  68.5 0.6 dynamic_slice.27
  70.9 0.7 fusion.99
  71.6 0.6 dynamic_slice.27
  74.0 0.7 fusion.99
  74.7 0.6 dynamic_slice.27
  77.1 0.7 fusion.99
  77.8 0.6 dynamic_slice.27
  80.2 0.7 fusion.99
  80.9 0.6 dynamic_slice.27
  83.3 0.7 fusion.99
  84.0 0.6 dynamic_slice.27
  86.4 0.7 fusion.99
  87.1 3.4 copy.29
  90.6 0.6 copy-done.1
  91.3 487.8 %all-reduce.21.cloned.1.call-done = f32[4096,192]{1,0:T(8,128)} async-done(((f32[4096,192]{1,0:T(8,128)}), f32[4096,192]{1,0:T(8,128)}) %all-reduce.21.cloned.1.call-update) | async-done | bytes 3145744 | tf_op jit(solution)/shard_map/psum | solution.py:149
  579.0 5.8 gather_fusion
  584.9 0.4 select_reduce_fusion
  585.3 2.5 fusion.17
  588.0 11.7 %cholesky.50 = f32[128,128]{1,0:T(8,128)S(1)} custom-call(f32[128,128]{1,0:T(8,128)S(1)} %cholesky.121), custom_call_target="Cholesky" | custom-call | tf_op jit(solution)/shard_map/jit(cholesky)/cholesky | solution.py:68
  599.8 0.9 fusion.19
  600.6 0.6 compare_reduce_fusion.1
  601.3 9.8 %custom-call.15 = f32[1,128,128]{1,2,0:T(8,128)S(1)} custom-call(f32[1,128,128]{2,1,0:T(8,128)S(1)} %get-tuple-element.153), custom_call_target="InvertDiagBlocksLowerTriangular" | custom-call | tf_op jit(solution)/shard_map/jit(cholesky)/cholesky | solution.py:68
  611.1 0.2 constant_dynamic-update-slice_fusion.3
  611.3 0.2 convolution_subtract_fusion.1
  611.5 5.8 cholesky.108
  617.3 0.6 compare_reduce_fusion
  619.4 19.9 %custom-call.16 = f32[2,128,128]{1,2,0:T(8,128)S(1)} custom-call(f32[2,128,128]{2,1,0:T(8,128)S(1)} %pad_maximum_fusion.2), custom_call_target="InvertDiagBlocksLowerTriangular" | custom-call | tf_op jit(solution)/shard_map/jit(_solve_triangular)/triangular_solve | solution.py:69
  639.3 0.3 fusion.59
  639.6 0.3 convolution_subtract_fusion
  639.9 0.3 fusion.69
  640.3 0.2 convolution_bitcast_fusion.1
  640.5 0.2 fusion.42
  640.7 1.3 convolution_add_fusion
  642.1 12.7 %all-to-all-start.1 = ((f32[192,1,128]{2,1,0:T(1,128)}), f32[192,1,128]{2,1,0:T(1,128)S(1)}, u32[]{:S(2)}, u32[]{:S(2)}) async-start(f32[192,1,128]{2,1,0:T(1,128)} %bitcast.21), calls=%async_computation.1 | async-start | bytes 196608 | tf_op jit(solution)/shard_map/all_to_all | solution.py:156
  654.8 1.3 constant_dynamic-slice_fusion
  656.1 12.8 %all-to-all-done.1 = f32[192,1,128]{2,1,0:T(1,128)S(1)} async-done(((f32[192,1,128]{2,1,0:T(1,128)}), f32[192,1,128]{2,1,0:T(1,128)S(1)}, u32[]{:S(2)}, u32[]{:S(2)}) %all-to-all-start.1) | async-done | bytes 98336 | tf_op jit(solution)/shard_map/all_to_all | solution.py:156
  668.9 0.6 copy.39
  (70 shorter events, 1.8 us)
Async XLA Ops:
  8.0 16.1 %collective-permute-start = (f32[12,4,128]{2,0,1:T(8,128)S(1)}, f32[12,4,128]{2,0,1:T(8,128)S(1)}, u32[]{:S(2)}, u32[]{:S(2)}) collective-permute-start(f32[12,4,128]{2,0,1:T(8,128)S(1)} %copy.37), channel_id=1, source_target_pairs={{0,1},{1,2},{2,3},{3,4},{4,5},{5,6},{6,7},{7,8},{8,9},{9,10},{10,1... | collective-permute-start | bytes 73736 | tf_op jit(solution)/shard_map/ppermute | solution.py:23
  13.0 12.1 %collective-permute-start.1 = (f32[12,4,128]{2,0,1:T(8,128)S(1)}, f32[12,4,128]{2,0,1:T(8,128)S(1)}, u32[]{:S(2)}, u32[]{:S(2)}) collective-permute-start(f32[12,4,128]{2,0,1:T(8,128)S(1)} %copy.38), channel_id=1, source_target_pairs={{1,0},{2,1},{3,2},{4,3},{5,4},{6,5},{7,6},{8,7},{9,8},{10,9},{11,1... | collective-permute-start | bytes 73736 | tf_op jit(solution)/shard_map/ppermute | solution.py:24
  19.7 5.3 collective-permute-start.2
  21.7 5.6 collective-permute-start.3
  29.6 16.2 %copy-start = (s32[2,4096]{1,0:T(2,128)S(1)}, s32[2,4096]{1,0:T(2,128)}, u32[]{:S(2)}) copy-start(s32[2,4096]{1,0:T(2,128)} %param.14) | copy-start | bytes 98308
  31.1 31.2 %all-to-all-start = ((f32[12,16,128]{2,0,1:T(8,128)}), f32[12,16,128]{2,0,1:T(8,128)S(1)}, u32[]{:S(2)}, u32[]{:S(2)}) async-start(f32[12,16,128]{2,0,1:T(8,128)} %slice_add_fusion.8), calls=%async_computation | async-start | bytes 262144 | tf_op jit(solution)/shard_map/all_to_all | solution.py:117
  45.7 533.3 %all-reduce.21.cloned.1.call-start = ((), (), s32[]{:S(2)}) async-start(), calls=%async_computation.2 | async-start | bytes 8388608 | tf_op jit(solution)/shard_map/psum | solution.py:149
  90.5 0.7 copy-start.1
  90.5 0.7 copy-start.2
  91.3 494.0 %copy-start.3 = (f32[1024]{0:T(1024)S(1)}, f32[1024]{0:T(1024)}, u32[]{:S(2)}) copy-start(f32[1024]{0:T(1024)} %param.16) | copy-start | bytes 12292
  642.1 26.8 %all-to-all-start.1 = ((f32[192,1,128]{2,1,0:T(1,128)}), f32[192,1,128]{2,1,0:T(1,128)S(1)}, u32[]{:S(2)}, u32[]{:S(2)}) async-start(f32[192,1,128]{2,1,0:T(1,128)} %bitcast.21), calls=%async_computation.1 | async-start | bytes 196608 | tf_op jit(solution)/shard_map/all_to_all | solution.py:156
Sparse Core Ops, SparseCore 0:
  90.6 488.3 all-reduce.20
where the time goes:
time: 678 us; the launch traced here: 676 us
  waiting for transfers between devices  518 us (76%)
  other arithmetic  55.2 us (8%)
  starting transfers between devices  41.8 us (6%)
  local copies, waits for them, and re-layouts  19.3 us (3%)
  between operations  15.8 us (2%)
  loops' own time  13.8 us (2%)
  matrix products  12.1 us (2%)
    psum x1, waiting for transfers between devices, shards(): lax.psum(lax.map(pixel_block, offsets).reshape(pixel_total, sample_vector...  488 us
    another operation x7, other arithmetic, finish(): factor = jnp.linalg.cholesky(gram)  28.7 us
    another operation x6, other arithmetic, finish(): inverse = jax.scipy.linalg.solve_triangular(factor, ident, lower=True)  20 us
    all_to_all x1, waiting for transfers between devices, shards(): lax.all_to_all(predicted_ensemble, 'member', split_axis=1, concat_axis=0,...  15.7 us
    all_to_all x1, starting transfers between devices, shards(): lax.all_to_all(predicted_ensemble, 'member', split_axis=1, concat_axis=0,...  14.7 us
    another operation x1, loops' own time, shards(): lax.map(pixel_block, offsets).reshape(pixel_total, sample_vectors)  13.8 us
  transfers between devices with their start and end apart: 7, of which 4 were waited for; matrix products, arithmetic and copies ran while one was open for 1% of the time, Pallas kernels for 0%

commit v1 on v0

v1 whole, which is shorter than its diff:
```python
import math

import jax
import jax.numpy as jnp
from jax import lax
from jax.experimental import pallas as pl
from jax.experimental.pallas import tpu as pltpu
from jax.sharding import PartitionSpec as P

STEPS = 4
time_step = 0.15
pixel_span = 64.0
top_depth = 2.0
F32 = jnp.float32
BF16 = jnp.bfloat16
HIGHEST = lax.Precision.HIGHEST
BLOCK = 256


def padded(value, sides, width):
    for axis, dim in sides:
        size, length = (lax.axis_size(axis), value.shape[dim])
        up = [(i, (i + 1) % size) for i in range(size - 1)]
        down = [(j, i) for i, j in up]
        last = lax.slice_in_dim(value, length - width, length, axis=dim)
        initial = lax.slice_in_dim(value, 0, width, axis=dim)
        before = lax.ppermute(last, axis, up)
        after = lax.ppermute(initial, axis, down)
        value = jnp.concatenate([before, value, after], axis=dim)
    return value


def advance_in_time(fluid_head_grid, perm_field, source, open_faces):
    mobility = perm_field * (1.0 + 0.5 * jnp.tanh(fluid_head_grid))
    sample_vectors, height, across_cells = fluid_head_grid.shape
    across = 0.5 * (mobility[:, 1:] + mobility[:, :-1]) * open_faces[None, :, None]
    flux_rows = across * (fluid_head_grid[:, 1:] - fluid_head_grid[:, :-1])
    zero_row = jnp.zeros((sample_vectors, 1, across_cells), fluid_head_grid.dtype)
    inflow = jnp.concatenate([flux_rows, zero_row], 1) - jnp.concatenate([zero_row, flux_rows], 1)
    along = 0.5 * (mobility[:, :, 1:] + mobility[:, :, :-1])
    flux_cols = along * (fluid_head_grid[:, :, 1:] - fluid_head_grid[:, :, :-1])
    zero_col = jnp.zeros((sample_vectors, height, 1), fluid_head_grid.dtype)
    inflow = inflow + (
        jnp.concatenate([flux_cols, zero_col], 2) - jnp.concatenate([zero_col, flux_cols], 2)
    )
    return fluid_head_grid + time_step * (inflow + source[None])


def face_mask(first_global, height, total_rows):
    index = first_global + jnp.arange(height - 1, dtype=jnp.int32)
    return ((index >= 0) & (index + 1 <= total_rows - 1)).astype(jnp.float32)


def split(value):
    high = value.astype(BF16)
    return high, (value - high.astype(F32)).astype(BF16)


def twice(value):
    return jnp.concatenate([value, value], axis=1)


def subsidence_kernel(volume, row_pitch, col_pitch, f_ref, lay_ref, pc_ref, out_ref, w_ref, h2_ref, vh_ref):
    slab = lax.axis_index("slab")
    members = f_ref.shape[0]
    rows, cols = lay_ref.shape
    high, low = split(f_ref[...])
    w_ref[...] = jnp.zeros_like(w_ref)
    w_ref[0:members, :] = high
    w_ref[16 : 16 + members, :] = low
    depth = top_depth + lay_ref[...].astype(F32)
    depth = jnp.concatenate([depth, jnp.zeros((cols - rows, cols), F32)], axis=0).T
    for i in range(rows):
        column = depth[:, i : i + 1]
        h2_ref[i] = jnp.broadcast_to(column * column, (cols, 128))
        vh_ref[i] = jnp.broadcast_to(volume * column, (cols, 128))
    cell_y = (lax.broadcasted_iota(jnp.int32, (cols, BLOCK), 0).astype(F32) + 0.5) * col_pitch
    first = (slab * rows).astype(F32)

    def block(b, carry):
        at = pl.multiple_of(b * BLOCK, BLOCK)
        coords = pc_ref[:, pl.ds(at, BLOCK)].astype(F32)
        delta_y = cell_y - coords[1:2]
        dy2 = delta_y * delta_y
        total = jnp.zeros((32, BLOCK), F32)
        for pair in range(rows // 2):
            tiles = []
            for i in (2 * pair, 2 * pair + 1):
                delta_x = (first + (i + 0.5)) * row_pitch - coords[0:1]
                radius = (dy2 + delta_x * delta_x) + twice(h2_ref[i])
                inv = lax.rsqrt(radius)
                tiles.append(twice(vh_ref[i]) * (inv * inv * inv))
            high, low = split(jnp.concatenate(tiles, axis=0))
            weights = w_ref[:, 256 * pair : 256 * pair + 256]
            total += jnp.dot(weights, high, preferred_element_type=F32)
            total += jnp.dot(weights, low, preferred_element_type=F32)
        out_ref[:, pl.ds(at, BLOCK)] = total[0:16] + total[16:32]
        return carry

    lax.fori_loop(0, pc_ref.shape[1] // BLOCK, block, 0)


def subsidence_partial(forecast, cell_layer, coords, total_rows):
    members, rows, cols = forecast.shape
    pixels = coords.shape[1]
    volume = pixel_span * pixel_span / (total_rows * cols)
    body = lambda *refs: subsidence_kernel(volume, pixel_span / total_rows, pixel_span / cols, *refs)
    return pl.pallas_call(
        body,
        name="subsidence",
        out_shape=jax.ShapeDtypeStruct((16, pixels), F32),
        in_specs=[pl.BlockSpec(memory_space=pltpu.VMEM)] * 3,
        out_specs=pl.BlockSpec(memory_space=pltpu.VMEM),
        scratch_shapes=[
            pltpu.VMEM((32, rows * cols), BF16),
            pltpu.VMEM((rows, cols, 128), F32),
            pltpu.VMEM((rows, cols, 128), F32),
        ],
    )(forecast.reshape(members, rows * cols), cell_layer, coords)


def mm(a, b):
    return jnp.dot(a, b, precision=HIGHEST, preferred_element_type=F32)


def mm_tn(a, b):
    return lax.dot_general(a, b, (((0,), (0,)), ((), ())), precision=HIGHEST, preferred_element_type=F32)


def inverse_factor(block):
    size = block.shape[0]
    row = lax.broadcasted_iota(jnp.int32, (size, 2 * size), 0)
    col = lax.broadcasted_iota(jnp.int32, (size, 2 * size), 1)
    work = jnp.concatenate([block, jnp.zeros_like(block)], axis=1)
    work = jnp.where(col == row + size, 1.0, work)
    for k in range(size - 1):
        pivot = work[k : k + 1, k : k + 1]
        factor = jnp.where(row[:, 0:1] > k, work[:, k : k + 1] / pivot, 0.0)
        work = work - factor * work[k : k + 1, :]
    diagonal = jnp.sum(jnp.where(col == row, work, 0.0), axis=1, keepdims=True)
    return work[:, size:] * lax.rsqrt(diagonal)


def transform_kernel(g_ref, m_ref):
    members = g_ref.shape[0]
    size = members // 3
    row = lax.broadcasted_iota(jnp.int32, (members, members), 0)
    col = lax.broadcasted_iota(jnp.int32, (members, members), 1)
    gram = g_ref[:, 0:members] + jnp.where(row == col, members - 1.0, 0.0)
    rhs = g_ref[:, members : members + 1]
    l0 = inverse_factor(gram[0:size, 0:size])
    t0 = mm(l0, gram[0:size, size:])
    s1 = gram[size:, size:] - mm_tn(t0, t0)
    z1 = -mm_tn(t0, l0)
    l1 = inverse_factor(s1[0:size, 0:size])
    t1 = mm(l1, s1[0:size, size:])
    l10 = mm(l1, z1[0:size])
    s2 = s1[size:, size:] - mm_tn(t1, t1)
    z2 = jnp.concatenate([z1[size:] - mm_tn(t1, l10), -mm_tn(t1, l1)], axis=1)
    l2 = inverse_factor(s2)
    l20 = mm(l2, z2)
    zero = jnp.zeros((size, size), F32)
    inverse = jnp.concatenate(
        [
            jnp.concatenate([l0, zero, zero], axis=1),
            jnp.concatenate([l10, l1, zero], axis=1),
            jnp.concatenate([l20, l2], axis=1),
        ],
        axis=0,
    )
    reduced = mm(inverse, rhs)
    weights = jnp.sum(inverse * reduced, axis=0, keepdims=True)
    m_ref[...] = weights + math.sqrt(members - 1.0) * inverse


def transform(gram):
    members = gram.shape[0]
    return pl.pallas_call(
        transform_kernel,
        name="transform",
        out_shape=jax.ShapeDtypeStruct((members, members), F32),
        in_specs=[pl.BlockSpec(memory_space=pltpu.VMEM)],
        out_specs=pl.BlockSpec(memory_space=pltpu.VMEM),
    )(gram)


def shards(
    fluid_head_start,
    conductivity_matrix,
    well_rates,
    cell_layer,
    pixel_coords,
    obs_index,
    obs_value,
    obs_sigma,
):
    local_members, slab_rows, across_cells = fluid_head_start.shape
    member_count = lax.axis_size("member")
    slab_count = lax.axis_size("slab")
    slab_index = lax.axis_index("slab")
    member_index = lax.axis_index("member")
    total_rows = slab_rows * slab_count
    members = local_members * member_count
    static = jnp.concatenate([conductivity_matrix, well_rates[None]], 0)
    static_ext = padded(static, (("slab", 1),), STEPS)
    grid = padded(fluid_head_start, (("slab", 1),), STEPS)
    open_faces = face_mask(slab_index * slab_rows - STEPS, slab_rows + 2 * STEPS, total_rows)
    for repeat in range(STEPS):
        grid = advance_in_time(grid, static_ext[:-1], static_ext[-1], open_faces)
    forecast = grid[:, STEPS : STEPS + slab_rows]
    collected = lax.all_to_all(forecast, "member", split_axis=1, concat_axis=0, tiled=True)
    pile = collected.reshape(members, -1)

    pixels = pixel_coords.shape[1]
    own = pixels // (member_count * slab_count)
    shape = (-1, member_count, slab_count, own)
    coords = pixel_coords.reshape(shape).transpose(0, 2, 1, 3).reshape(-1, pixels)
    partial = subsidence_partial(forecast, cell_layer, coords, total_rows)[:local_members]
    chunk = pixels // slab_count
    partial = partial.reshape(local_members, slab_count, chunk).transpose(1, 0, 2)
    mine = lax.psum_scatter(partial, "slab", scatter_dimension=0, tiled=True)[0]
    predicted = lax.all_gather(mine, "member", axis=0, tiled=True)
    own_part = lax.dynamic_slice_in_dim(predicted, member_index * own, own, 1).T

    position = jnp.arange(chunk, dtype=jnp.int32)
    pixel = (position // own * slab_count + slab_index) * own + position % own
    hit = obs_index[:, None] == pixel[None, :]
    inverse_var = 1.0 / (obs_sigma * obs_sigma)
    sums = jnp.dot(
        jnp.stack([inverse_var, inverse_var * obs_value]), hit.astype(F32), precision=HIGHEST
    )
    centre = jnp.mean(predicted, axis=0)
    anomaly = predicted - centre[None]
    weighted = jnp.concatenate([anomaly * sums[0:1], (sums[1] - sums[0] * centre)[None]], 0)
    gram = lax.dot_general(anomaly, weighted, (((1,), (1,)), ((), ())), precision=HIGHEST)
    mix = transform(lax.psum(gram, "slab"))

    centre = jnp.mean(pile, axis=0)
    analysed = centre[None] + jnp.dot(mix, pile - centre[None], precision=HIGHEST)
    analysed = analysed.reshape(collected.shape)
    returned = lax.all_to_all(analysed, "member", split_axis=0, concat_axis=1, tiled=True)
    return (returned, own_part)


def solution(mesh):
    return jax.shard_map(
        shards,
        mesh=mesh,
        in_specs=(
            P("member", "slab", None),
            P("member", "slab", None),
            P("slab", None),
            P("slab", None),
            P(),
            P(),
            P(),
            P(),
        ),
        out_specs=(P("member", "slab", None), P(("member", "slab"), None)),
        check_vma=False,
    )
```

time: 678 us -> 714 us (1.053)
  other arithmetic: 55.2 us -> 2.66 us
  blocking collectives: 0 us -> 44.8 us
  waiting for transfers between devices: 518 us -> 558 us
  Pallas kernels: 0 us -> 34.3 us
  loops' own time: 13.8 us -> 0 us
  matrix products: 12.1 us -> 2.36 us
  local copies, waits for them, and re-layouts: 19.3 us -> 11.7 us
    unnamed x1 -> x3, waiting for transfers between devices: 0.02 us -> 268 us
    psum x1, waiting for transfers between devices: 488 us -> 277 us  [shards(): mix = transform(lax.psum(gram, 'slab'))]
    another operation x13 -> x0, other arithmetic: 48.7 us -> none  [the longest x7 28.7 us: finish(): factor = jnp.linalg.cholesky(gram)]
    all_gather x0 -> x1, blocking collectives: none -> 44.8 us  [shards(): predicted = lax.all_gather(mine, 'member', axis=0, tiled=True)]
    pallas_call x0 -> x2, Pallas kernels: none -> 34.3 us  [the longest x1 19.3 us: transform(): pl.pallas_call(transform_kernel, name='transform', out_shape=jax.ShapeDty...]
    all_to_all x1, waiting for transfers between devices: 15.7 us -> 0.01 us  [shards(): lax.all_to_all(forecast, 'member', split_axis=1, concat_axis=0, tiled=True)]
    another operation x1 -> x0, loops' own time: 13.8 us -> none  [shards(): lax.map(pixel_block, offsets).reshape(pixel_total, sample_vectors)]
    dot_general x13 -> x3, matrix products: 10.8 us -> 2.36 us  [the longest x1 1.03 us: shards(): lax.dot_general(anomaly, weighted, (((1,), (1,)), ((), ())), precision=HI...]
  transfers between devices with their start and end apart: 7 -> 8, of which waited for: 4 -> 4; matrix products, arithmetic and copies ran while one was open for 1% -> 1% of each run, Pallas kernels for 0% -> 3%
where the time goes in v1:
time: 714 us; the launch traced here: 710 us
  waiting for transfers between devices  558 us (78%)
  blocking collectives  44.8 us (6%)
  starting transfers between devices  41.4 us (6%)
  Pallas kernels  34.3 us (5%)
  between operations  14.4 us (2%)
  local copies, waits for them, and re-layouts  11.7 us (2%)
    psum x1, waiting for transfers between devices, shards(): mix = transform(lax.psum(gram, 'slab'))  277 us
    unnamed x3, waiting for transfers between devices  268 us
    all_gather x1, blocking collectives, shards(): predicted = lax.all_gather(mine, 'member', axis=0, tiled=True)  44.8 us
    pallas_call x1, Pallas kernels, transform(): pl.pallas_call(transform_kernel, name='transform', out_shape=jax.ShapeDty...  19.3 us
    pallas_call x1, Pallas kernels, subsidence_partial(): pl.pallas_call(body, name='subsidence', out_shape=jax.ShapeDtypeStruct((1...  15 us
    all_to_all x1, starting transfers between devices, shards(): lax.all_to_all(forecast, 'member', split_axis=1, concat_axis=0, tiled=True)  14.7 us
  transfers between devices with their start and end apart: 8, of which 4 were waited for; matrix products, arithmetic and copies ran while one was open for 1% of the time, Pallas kernels for 3%

profile of v1, /device:TPU:1, one launch (start us, length us, event | category | flops | bytes accessed | tf_op | source)
XLA Modules:
  0.0 709.8 jit_solution(1966328407337014386)
XLA Ops:
  7.2 0.0 copy-start.2
  7.2 0.0 all-reduce.22.cloned.1.call-start
  7.2 0.8 fusion.42
  8.1 4.9 collective-permute-start
  13.0 0.0 copy-start.3
  13.0 5.1 collective-permute-start.1
  18.1 0.0 copy-done.2
  18.2 0.0 copy-done.3
  18.2 0.0 copy-start.5
  18.2 0.0 copy-start.6
  18.3 0.0 copy-start.4
  18.3 1.9 collective-permute-start.2
  20.2 2.4 collective-permute-start.3
  22.6 0.0 copy-done.5
  22.6 0.0 copy-done.6
  22.7 0.0 copy-done.4
  22.7 0.3 reshape.71
  23.0 0.3 copy.35
  23.3 0.0 copy-start.1
  23.3 0.9 reshape.72.refs_2_
  24.2 1.3 dynamic-slice.1
  25.5 0.0 collective-permute-done
  25.6 0.0 collective-permute-done.1
  25.6 0.0 collective-permute-done.2
  25.6 0.2 collective-permute-done.3
  25.9 0.2 fusion.10
  26.1 0.1 fusion.18
  26.2 0.1 add_multiply_fusion.2
  26.3 0.1 fusion.16
  26.4 0.2 fusion.8
  26.6 0.1 add_multiply_fusion.1
  26.7 0.1 fusion.14
  26.8 0.2 fusion.6
  27.0 0.1 add_multiply_fusion
  27.2 0.1 fusion.12
  27.3 0.2 fusion.4
  27.4 0.8 slice_add_fusion.8
  28.2 0.9 copy.34
  29.2 0.7 copy.42
  29.9 15.0 %subsidence.1 = f32[16,4096]{1,0:T(8,128)} custom-call(f32[12,2048]{1,0:T(8,128)} %bitcast.49, s32[16,128]{1,0:T(8,128)} %refs_1_.1, s32[2,4096]{1,0:T(2,128)} %reshape.72.refs_2_), custom_call_target="tpu_custom_call" | custom-call | tf_op jit(solution)/shard_map/subsidence/pallas_call | solution.py:108
  44.8 1.0 copy.43
  45.8 0.7 slice_bitcast_fusion
  46.5 0.0 all-reduce.22.cloned.1.call-update
  46.6 0.0 copy-start.7
  46.6 0.7 copy-done.7
  47.2 0.4 fusion
  47.6 14.7 %all-to-all-start = ((f32[12,16,128]{2,0,1:T(8,128)}), f32[12,16,128]{2,0,1:T(8,128)S(1)}, u32[]{:S(2)}, u32[]{:S(2)}) async-start(f32[12,16,128]{2,0,1:T(8,128)} %slice_add_fusion.8), calls=%async_computation | async-start | bytes 262144 | tf_op jit(solution)/shard_map/all_to_all | solution.py:211
  62.3 0.0 all-reduce.20.cloned.1.call-start
  62.4 268.2 %all-reduce.22.cloned.1.call-done = f32[32,12,128]{2,0,1:T(8,128)} async-done(((f32[32,12,128]{2,0,1:T(8,128)}), f32[32,12,128]{2,0,1:T(8,128)}) %all-reduce.22.cloned.1.call-update) | async-done | bytes 196624
  330.5 1.5 constant_dynamic-slice_fusion
  332.0 44.8 %all-gather = f32[1,192,128]{2,0,1:T(1,128)S(1)} all-gather(f32[1,12,128]{2,0,1:T(1,128)S(1)} %constant_dynamic-slice_fusion), channel_id=2, replica_groups=mesh['member'=16,'slab'=32] {'member'}, dimensions={1}, use_global_device_ids=true | all-gather | bytes 104448 | tf_op jit(solution)/shard_map/all_gather | solution.py:222
  376.8 0.2 reduce_sum.19
  377.1 1.0 fusion.23
  378.1 0.0 all-reduce.20.cloned.1.call-update
  378.1 276.7 %all-reduce.20.cloned.1.call-done.g_ref = f32[192,193]{1,0:T(8,128)} async-done(((f32[192,193]{1,0:T(8,128)}), f32[192,193]{1,0:T(8,128)}) %all-reduce.20.cloned.1.call-update) | async-done | bytes 148240 | tf_op jit(solution)/shard_map/psum | solution.py:236
  654.8 19.3 %transform.1 = f32[192,192]{1,0:T(8,128)} custom-call(f32[192,193]{1,0:T(8,128)} %all-reduce.20.cloned.1.call-done.g_ref), custom_call_target="tpu_custom_call" | custom-call | tf_op jit(solution)/shard_map/transform/pallas_call | solution.py:178
  674.1 0.0 all-to-all-done
  674.2 0.9 copy-done
  675.0 1.0 convolution_add_fusion
  676.0 12.3 %all-to-all-start.1 = ((f32[192,1,128]{2,1,0:T(1,128)}), f32[192,1,128]{2,1,0:T(1,128)S(1)}, u32[]{:S(2)}, u32[]{:S(2)}) async-start(f32[192,1,128]{2,1,0:T(1,128)} %bitcast.12), calls=%async_computation.1 | async-start | bytes 196608 | tf_op jit(solution)/shard_map/all_to_all | solution.py:241
  688.3 0.3 constant_dynamic-slice_fusion.1
  688.5 0.7 copy.41
  689.2 13.1 %all-to-all-done.1 = f32[192,1,128]{2,1,0:T(1,128)S(1)} async-done(((f32[192,1,128]{2,1,0:T(1,128)}), f32[192,1,128]{2,1,0:T(1,128)S(1)}, u32[]{:S(2)}, u32[]{:S(2)}) %all-to-all-start.1) | async-done | bytes 98336 | tf_op jit(solution)/shard_map/all_to_all | solution.py:241
  702.3 0.6 copy.48
  (23 shorter events, 0.3 us)
Async XLA Ops:
  7.2 11.0 %copy-start.2 = (f32[12,16,128]{2,1,0:T(8,128)S(1)}, f32[12,16,128]{2,1,0:T(8,128)}, u32[]{:S(2)}) copy-start(f32[12,16,128]{2,1,0:T(8,128)} %param.9) | copy-start | bytes 294916
  7.2 323.4 %all-reduce.22.cloned.1.call-start = ((), (), s32[]{:S(2)}) async-start(), calls=%async_computation.3 | async-start | bytes 393216
  8.1 17.4 %collective-permute-start = (f32[12,4,128]{2,0,1:T(8,128)S(1)}, f32[12,4,128]{2,0,1:T(8,128)S(1)}, u32[]{:S(2)}, u32[]{:S(2)}) collective-permute-start(f32[12,4,128]{2,0,1:T(8,128)S(1)} %copy.46), channel_id=1, source_target_pairs={{0,1},{1,2},{2,3},{3,4},{4,5},{5,6},{6,7},{7,8},{8,9},{9,10},{10,1... | collective-permute-start | bytes 73736 | tf_op jit(solution)/shard_map/ppermute | solution.py:27
  13.0 5.2 copy-start.3
  13.0 12.5 %collective-permute-start.1 = (f32[12,4,128]{2,0,1:T(8,128)S(1)}, f32[12,4,128]{2,0,1:T(8,128)S(1)}, u32[]{:S(2)}, u32[]{:S(2)}) collective-permute-start(f32[12,4,128]{2,0,1:T(8,128)S(1)} %copy.47), channel_id=1, source_target_pairs={{1,0},{2,1},{3,2},{4,3},{5,4},{6,5},{7,6},{8,7},{9,8},{10,9},{11,1... | collective-permute-start | bytes 73736 | tf_op jit(solution)/shard_map/ppermute | solution.py:28
  18.2 4.4 copy-start.5
  18.2 4.4 copy-start.6
  18.3 4.4 copy-start.4
  18.3 7.3 %collective-permute-start.2 = (f32[13,4,128]{2,0,1:T(8,128)S(1)}, f32[13,4,128]{2,0,1:T(8,128)S(1)}, u32[]{:S(2)}, u32[]{:S(2)}) collective-permute-start(f32[13,4,128]{2,0,1:T(8,128)S(1)} %get-tuple-element.10), channel_id=1, source_target_pairs={{0,1},{1,2},{2,3},{3,4},{4,5},{5,6},{6,7},{7,8},{8,9},{9,10},{10,1... | collective-permute-start | bytes 79880 | tf_op jit(solution)/shard_map/ppermute | solution.py:27
  20.2 5.6 collective-permute-start.3
  23.3 2.2 copy-start.1
  46.6 0.7 copy-start.7
  47.6 626.5 %all-to-all-start = ((f32[12,16,128]{2,0,1:T(8,128)}), f32[12,16,128]{2,0,1:T(8,128)S(1)}, u32[]{:S(2)}, u32[]{:S(2)}) async-start(f32[12,16,128]{2,0,1:T(8,128)} %slice_add_fusion.8), calls=%async_computation | async-start | bytes 262144 | tf_op jit(solution)/shard_map/all_to_all | solution.py:211
  62.3 592.5 %all-reduce.20.cloned.1.call-start = ((), (), s32[]{:S(2)}) async-start(), calls=%async_computation.2 | async-start | bytes 393216 | tf_op jit(solution)/shard_map/psum | solution.py:236
  674.1 0.9 copy-start
  676.0 26.3 %all-to-all-start.1 = ((f32[192,1,128]{2,1,0:T(1,128)}), f32[192,1,128]{2,1,0:T(1,128)S(1)}, u32[]{:S(2)}, u32[]{:S(2)}) async-start(f32[192,1,128]{2,1,0:T(1,128)} %bitcast.12), calls=%async_computation.1 | async-start | bytes 196608 | tf_op jit(solution)/shard_map/all_to_all | solution.py:241
Sparse Core Ops, SparseCore 0:
  46.7 283.8 all-reduce.21
  378.3 276.4 all-reduce.19

commit v2 on v1

v2 whole, which is shorter than its diff:
```python
import math

import jax
import jax.numpy as jnp
from jax import lax
from jax.experimental import pallas as pl
from jax.experimental.pallas import tpu as pltpu
from jax.sharding import PartitionSpec as P

STEPS = 4
time_step = 0.15
pixel_span = 64.0
top_depth = 2.0
F32 = jnp.float32
BF16 = jnp.bfloat16
HIGHEST = lax.Precision.HIGHEST
MESH = pl.DeviceIdType.MESH
BLOCK = 256
LANES = 128
EARLY = 10


def split(value):
    high = value.astype(BF16)
    return high, (value - high.astype(F32)).astype(BF16)


def twice(value):
    return jnp.concatenate([value, value], axis=1)


def dot(a, b, dims):
    return lax.dot_general(a, b, (dims, ((), ())), precision=HIGHEST, preferred_element_type=F32)


def mm(a, b):
    return dot(a, b, ((1,), (0,)))


def mm_tn(a, b):
    return dot(a, b, ((0,), (0,)))


def mm_nt(a, b):
    return dot(a, b, ((1,), (1,)))


def inverse_factor(block):
    size = block.shape[0]
    row = lax.broadcasted_iota(jnp.int32, (size, 2 * size), 0)
    col = lax.broadcasted_iota(jnp.int32, (size, 2 * size), 1)
    work = jnp.concatenate([block, jnp.zeros_like(block)], axis=1)
    work = jnp.where(col == row + size, 1.0, work)
    for k in range(size - 1):
        line = work[k : k + 1, :]
        scaled = line * (1.0 / work[k : k + 1, k : k + 1])
        factor = jnp.where(row[:, 0:1] > k, work[:, k : k + 1], 0.0)
        work = work - factor * scaled
    diagonal = jnp.sum(jnp.where(col == row, work, 0.0), axis=1, keepdims=True)
    return work[:, size:] * lax.rsqrt(diagonal)


def transform(packed, rhs, members):
    size = members // 3
    row = lax.broadcasted_iota(jnp.int32, (members, 2 * size), 0)
    col = lax.broadcasted_iota(jnp.int32, (members, 2 * size), 1)
    gram = packed + jnp.where(row == col, members - 1.0, 0.0)
    corner = packed[0:size, size:] + jnp.where(row == col, members - 1.0, 0.0)[0:size, 0:size]
    l0 = inverse_factor(gram[0:size, 0:size])
    t0 = mm_nt(l0, gram[size:, 0:size])
    s1 = gram[size:, size:] - mm_tn(t0, t0[:, 0:size])
    z1 = -mm_tn(t0, l0)
    l1 = inverse_factor(s1[0:size])
    t1 = mm_nt(l1, s1[size:])
    l10 = mm(l1, z1[0:size])
    s2 = corner - mm_tn(t0[:, size:], t0[:, size:]) - mm_tn(t1, t1)
    z2 = jnp.concatenate([z1[size:] - mm_tn(t1, l10), -mm_tn(t1, l1)], axis=1)
    l2 = inverse_factor(s2)
    l20 = mm(l2, z2)
    zero = jnp.zeros((size, size), F32)
    inverse = jnp.concatenate(
        [
            jnp.concatenate([l0, zero, zero], axis=1),
            jnp.concatenate([l10, l1, zero], axis=1),
            jnp.concatenate([l20, l2], axis=1),
        ],
        axis=0,
    )
    reduced = jnp.sum(inverse * rhs, axis=1, keepdims=True)
    weights = jnp.sum(inverse * reduced, axis=0, keepdims=True)
    return weights + math.sqrt(members - 1.0) * inverse


def advance(head, perm, source, open_first, open_last, first_row, rows):
    mobility = perm * (1.0 + 0.5 * jnp.tanh(head))
    last = head.shape[0] - 1
    cols = head.shape[2]
    flux = 0.5 * (mobility[1:] + mobility[:-1]) * (head[1:] - head[:-1])
    parts = [flux[i : i + 1] for i in range(last)]
    near, far = STEPS - 1 - first_row, STEPS - 1 + rows - first_row
    parts[near] = parts[near] * open_first
    parts[far] = parts[far] * open_last
    flux = jnp.concatenate(parts, axis=0)
    inner = head[1:-1]
    own = mobility[1:-1]
    lane = lax.broadcasted_iota(jnp.int32, inner.shape, 2)
    along = 0.5 * (jnp.roll(own, -1, axis=2) + own) * (jnp.roll(inner, -1, axis=2) - inner)
    along = jnp.where(lane < cols - 1, along, 0.0)
    back = jnp.where(lane > 0, jnp.roll(along, 1, axis=2), 0.0)
    inflow = (flux[1:] - flux[:-1]) + (along - back)
    return inner + time_step * (inflow + source[1:-1])


def cycle_kernel(
    total_rows,
    head_ref,
    cond_ref,
    well_ref,
    lay_ref,
    pc_ref,
    oi_ref,
    ov_ref,
    os_ref,
    ret_ref,
    own_ref,
    hx,
    cx,
    wx,
    fore,
    w_ref,
    h2_ref,
    vh_ref,
    khi,
    klo,
    part,
    rs,
    mine,
    ag,
    flat,
    turned,
    gpart,
    gred,
    gall,
    pile,
    snd,
    back,
    halo_s,
    halo_r,
    out_s,
    out_r,
    rs_s,
    rs_r,
    ag_s,
    ag_r,
    g1_s,
    g1_r,
    g2_s,
    g2_r,
    rt_s,
    rt_r,
):
    slab, member = lax.axis_index("slab"), lax.axis_index("member")
    slabs, groups = lax.axis_size("slab"), lax.axis_size("member")
    rows, local, cols = head_ref.shape
    members = local * groups
    blocks = pc_ref.shape[1] // BLOCK
    row_pitch, col_pitch = pixel_span / total_rows, pixel_span / cols
    volume = pixel_span * pixel_span / (total_rows * cols)

    def other(i, axis):
        me, n = (slab, slabs) if axis == "slab" else (member, groups)
        return lax.rem(me + i, n)

    def peers(axis, body):
        n = slabs if axis == "slab" else groups

        def step(i, carry):
            body(other(i, axis))
            return carry

        lax.fori_loop(1, n, step, 0)

    def copy(src, dst, ssem, rsem, axis, to):
        return pltpu.make_async_remote_copy(
            src_ref=src,
            dst_ref=dst,
            send_sem=ssem,
            recv_sem=rsem,
            device_id={axis: to},
            device_id_type=MESH,
        )

    barrier = pltpu.get_barrier_semaphore()
    for axis in ("slab", "member"):
        peers(
            axis,
            lambda to: pl.semaphore_signal(barrier, inc=1, device_id={axis: to}, device_id_type=MESH),
        )

    depth = top_depth + lay_ref[...].astype(F32)
    depth = jnp.concatenate([depth, jnp.zeros((cols - rows, cols), F32)], axis=0).T
    for i in range(rows):
        column = depth[:, i : i + 1]
        h2_ref[i] = jnp.broadcast_to(column * column, (cols, LANES))
        vh_ref[i] = jnp.broadcast_to(volume * column, (cols, LANES))
    cell_y = (lax.broadcasted_iota(jnp.int32, (cols, BLOCK), 0).astype(F32) + 0.5) * col_pitch
    first = (slab * rows).astype(F32)

    def evaluate(b, carry):
        at = pl.multiple_of(b * BLOCK, BLOCK)
        coords = pc_ref[:, pl.ds(at, BLOCK)].astype(F32)
        delta_y = cell_y - coords[1:2]
        dy2 = delta_y * delta_y
        for i in range(rows):
            delta_x = (first + (i + 0.5)) * row_pitch - coords[0:1]
            radius = (dy2 + delta_x * delta_x) + twice(h2_ref[i])
            inv = lax.rsqrt(radius)
            high, low = split(twice(vh_ref[i]) * (inv * inv * inv))
            khi[b, cols * i : cols * i + cols, :] = high
            klo[b, cols * i : cols * i + cols, :] = low
        return carry

    early = min(EARLY, blocks - 1)
    lax.fori_loop(0, early, evaluate, 0)

    pl.semaphore_wait(barrier, slabs - 1 + groups - 1)

    up, down = other(1, "slab"), other(slabs - 1, "slab")
    halos = []
    for n, (src, dst) in enumerate(((head_ref, hx), (cond_ref, cx), (well_ref, wx))):
        halos.append(
            copy(
                src.at[pl.ds(rows - STEPS, STEPS)],
                dst.at[pl.ds(0, STEPS)],
                halo_s.at[2 * n],
                halo_r.at[2 * n],
                "slab",
                up,
            )
        )
        halos.append(
            copy(
                src.at[pl.ds(0, STEPS)],
                dst.at[pl.ds(rows + STEPS, STEPS)],
                halo_s.at[2 * n + 1],
                halo_r.at[2 * n + 1],
                "slab",
                down,
            )
        )
    for item in halos:
        item.start()
    hx[STEPS : STEPS + rows] = head_ref[...]
    cx[STEPS : STEPS + rows] = cond_ref[...]
    wx[STEPS : STEPS + rows] = well_ref[...]
    lax.fori_loop(early, blocks, evaluate, 0)

    position = lax.broadcasted_iota(jnp.int32, (LANES, oi_ref.shape[1]), 0)
    own = LANES // groups
    pixel = ((position // own) * slabs + slab) * own + lax.rem(position, own)
    hit = jnp.where(oi_ref[...] == pixel, 1.0, 0.0)
    inverse_var = 1.0 / (os_ref[...] * os_ref[...])
    first_line = lax.broadcasted_iota(jnp.int32, (8, oi_ref.shape[1]), 0) == 0
    sums = mm_nt(jnp.where(first_line, inverse_var, inverse_var * ov_ref[...]), hit)

    for item in halos:
        item.wait_recv()
    head, perm, source = hx[...], cx[...], wx[...]
    open_first = jnp.where(slab == 0, 0.0, 1.0)
    open_last = jnp.where(slab == slabs - 1, 0.0, 1.0)
    for k in range(STEPS):
        head = advance(head, perm, source, open_first, open_last, k, rows)
        perm, source = perm[1:-1], source[1:-1]
    fore[...] = head
    w_ref[...] = jnp.zeros_like(w_ref)
    for i in range(rows):
        high, low = split(head[i])
        w_ref[0:local, cols * i : cols * i + cols] = high
        w_ref[16 : 16 + local, cols * i : cols * i + cols] = low

    peers(
        "member",
        lambda to: copy(
            fore.at[to], pile.at[member], out_s.at[to], out_r.at[member], "member", to
        ).start(),
    )

    def product(n, carry):
        b = lax.rem(n + slab // 2, blocks)
        total = jnp.dot(w_ref[...], khi[b], preferred_element_type=F32)
        total += jnp.dot(w_ref[...], klo[b], preferred_element_type=F32)
        total = total[0:16] + total[16:32]
        for half in range(BLOCK // LANES):
            to = b * (BLOCK // LANES) + half
            part[to] = total[0:local, LANES * half : LANES * half + LANES]

            @pl.when(to != slab)
            def _():
                copy(part.at[to], rs.at[slab], rs_s.at[to], rs_r.at[slab], "slab", to).start()

        return carry

    lax.fori_loop(0, blocks, product, 0)

    def rs_wait(frm):
        copy(part.at[frm], rs.at[frm], rs_s.at[frm], rs_r.at[frm], "slab", frm).wait_recv()

    peers("slab", rs_wait)
    rs[slab] = part[slab]
    total = rs[0]
    for n in range(1, slabs):
        total += rs[n]
    ag[member] = total
    mine[...] = total
    peers(
        "member",
        lambda to: copy(mine, ag.at[member], ag_s.at[to], ag_r.at[member], "member", to).start(),
    )
    peers(
        "member",
        lambda frm: copy(mine, ag.at[frm], ag_s.at[frm], ag_r.at[frm], "member", frm).wait_recv(),
    )
    for n in range(groups):
        flat[local * n : local * n + local, :] = ag[n]
    predicted = flat[...]
    centre = jnp.sum(predicted, axis=0, keepdims=True) * (1.0 / members)
    anomaly = predicted - centre
    counts = sums[0:1]
    gram = mm_nt(anomaly, anomaly * counts)
    rhs = mm_nt(jnp.broadcast_to(sums[1:2] - counts * centre, (8, LANES)), anomaly)
    size = members // 3
    top = jnp.concatenate([gram[0:size, 0:size], gram[2 * size :, 2 * size :]], axis=1)
    pieces = [top, gram[size:, 0 : 2 * size], rhs[:, 0:LANES]]
    pieces.append(jnp.concatenate([rhs[:, LANES:], jnp.zeros((8, 2 * LANES - members), F32)], axis=1))
    height = gpart.shape[1]
    pieces.append(jnp.zeros((slabs * height - members - 16, LANES), F32))
    gpart[...] = jnp.concatenate(pieces, axis=0).reshape(slabs, height, LANES)
    peers(
        "slab",
        lambda to: copy(
            gpart.at[to], gred.at[slab], g1_s.at[to], g1_r.at[slab], "slab", to
        ).start(),
    )
    predicted = jnp.concatenate([predicted, jnp.zeros((2 * LANES - members, LANES), F32)], axis=0)
    turned[...] = predicted.T
    own_ref[...] = turned[pl.ds(pl.multiple_of(member * own, own), own), :][:, 0:members]
    peers(
        "slab",
        lambda frm: copy(
            gpart.at[frm], gred.at[frm], g1_s.at[frm], g1_r.at[frm], "slab", frm
        ).wait_recv(),
    )
    gred[slab] = gpart[slab]
    total = gred[0]
    for n in range(1, slabs):
        total += gred[n]
    gall[slab] = total
    peers(
        "slab",
        lambda to: copy(
            gall.at[slab], gall.at[slab], g2_s.at[to], g2_r.at[slab], "slab", to
        ).start(),
    )
    peers(
        "member",
        lambda frm: copy(
            fore.at[frm], pile.at[frm], out_s.at[frm], out_r.at[frm], "member", frm
        ).wait_recv(),
    )
    pile[member] = fore[member]
    for n in range(groups):
        flat[local * n : local * n + local, :] = pile[n]
    spread = flat[...]
    centre = jnp.sum(spread, axis=0, keepdims=True) * (1.0 / members)
    spread = spread - centre
    peers(
        "slab",
        lambda frm: copy(
            gall.at[frm], gall.at[frm], g2_s.at[frm], g2_r.at[frm], "slab", frm
        ).wait_recv(),
    )
    packed = gall[...].reshape(slabs * height, LANES)
    rhs = jnp.concatenate(
        [packed[members : members + 1], packed[members + 8 : members + 9]], axis=1
    )[:, 0:members]
    mix = transform(packed[0:members], rhs, members)
    flat[...] = centre + mm(mix, spread)
    for n in range(groups):
        snd[n] = flat[local * n : local * n + local, :]
    peers(
        "member",
        lambda to: copy(
            snd.at[to], back.at[member], rt_s.at[to], rt_r.at[member], "member", to
        ).start(),
    )
    back[member] = snd[member]
    peers(
        "member",
        lambda frm: copy(
            snd.at[frm], back.at[frm], rt_s.at[frm], rt_r.at[frm], "member", frm
        ).wait_recv(),
    )
    ret_ref[...] = back[...]

    for item in halos:
        item.wait_send()

    def drain_member(to):
        copy(fore.at[to], pile.at[to], out_s.at[to], out_r.at[to], "member", to).wait_send()
        copy(mine, ag.at[to], ag_s.at[to], ag_r.at[to], "member", to).wait_send()
        copy(snd.at[to], back.at[to], rt_s.at[to], rt_r.at[to], "member", to).wait_send()

    def drain_slab(to):
        copy(part.at[to], rs.at[to], rs_s.at[to], rs_r.at[to], "slab", to).wait_send()
        copy(gpart.at[to], gred.at[to], g1_s.at[to], g1_r.at[to], "slab", to).wait_send()
        copy(gall.at[slab], gall.at[to], g2_s.at[to], g2_r.at[to], "slab", to).wait_send()

    peers("member", drain_member)
    peers("slab", drain_slab)


def shards(
    fluid_head_start,
    conductivity_matrix,
    well_rates,
    cell_layer,
    pixel_coords,
    obs_index,
    obs_value,
    obs_sigma,
):
    local, rows, cols = fluid_head_start.shape
    groups = lax.axis_size("member")
    slabs = lax.axis_size("slab")
    members = local * groups
    pixels = pixel_coords.shape[1]
    own = pixels // (groups * slabs)
    height = 256 // slabs
    coords = pixel_coords.reshape(-1, groups, slabs, own).transpose(0, 2, 1, 3).reshape(-1, pixels)
    vmem = pl.BlockSpec(memory_space=pltpu.VMEM)
    dma = pltpu.SemaphoreType.DMA
    tall = rows + 2 * STEPS
    blocks = pixels // BLOCK
    body = lambda *refs: cycle_kernel(rows * slabs, *refs)
    returned, own_part = pl.pallas_call(
        body,
        name="cycle",
        out_shape=(
            jax.ShapeDtypeStruct((groups, local, cols), F32),
            jax.ShapeDtypeStruct((own, members), F32),
        ),
        in_specs=[vmem] * 8,
        out_specs=(vmem, vmem),
        scratch_shapes=[
            pltpu.VMEM((tall, local, cols), F32),
            pltpu.VMEM((tall, local, cols), F32),
            pltpu.VMEM((tall, 1, cols), F32),
            pltpu.VMEM((rows, local, cols), F32),
            pltpu.VMEM((32, rows * cols), BF16),
            pltpu.VMEM((rows, cols, LANES), F32),
            pltpu.VMEM((rows, cols, LANES), F32),
            pltpu.VMEM((blocks, rows * cols, BLOCK), BF16),
            pltpu.VMEM((blocks, rows * cols, BLOCK), BF16),
            pltpu.VMEM((slabs, local, LANES), F32),
            pltpu.VMEM((slabs, local, LANES), F32),
            pltpu.VMEM((local, LANES), F32),
            pltpu.VMEM((groups, local, LANES), F32),
            pltpu.VMEM((members, LANES), F32),
            pltpu.VMEM((LANES, 2 * LANES), F32),
            pltpu.VMEM((slabs, height, LANES), F32),
            pltpu.VMEM((slabs, height, LANES), F32),
            pltpu.VMEM((slabs, height, LANES), F32),
            pltpu.VMEM((groups, local, cols), F32),
            pltpu.VMEM((groups, local, cols), F32),
            pltpu.VMEM((groups, local, cols), F32),
            dma((6,)),
            dma((6,)),
            dma((groups,)),
            dma((groups,)),
            dma((slabs,)),
            dma((slabs,)),
            dma((groups,)),
            dma((groups,)),
            dma((slabs,)),
            dma((slabs,)),
            dma((slabs,)),
            dma((slabs,)),
            dma((groups,)),
            dma((groups,)),
        ],
        compiler_params=pltpu.CompilerParams(
            collective_id=0, has_side_effects=True, vmem_limit_bytes=60 * 1024 * 1024
        ),
    )(
        fluid_head_start.transpose(1, 0, 2),
        conductivity_matrix.transpose(1, 0, 2),
        well_rates[:, None, :],
        cell_layer,
        coords,
        obs_index[None],
        obs_value[None],
        obs_sigma[None],
    )
    return (returned.transpose(1, 0, 2), own_part)


def solution(mesh):
    return jax.shard_map(
        shards,
        mesh=mesh,
        in_specs=(
            P("member", "slab", None),
            P("member", "slab", None),
            P("slab", None),
            P("slab", None),
            P(),
            P(),
            P(),
            P(),
        ),
        out_specs=(P("member", "slab", None), P(("member", "slab"), None)),
        check_vma=False,
    )
```

time: 714 us -> 95.2 us (0.13)
  waiting for transfers between devices: 558 us -> 0 us
  Pallas kernels: 34.3 us -> 88.9 us
  blocking collectives: 44.8 us -> 0 us
  starting transfers between devices: 41.4 us -> 0 us
  between operations: 14.4 us -> 0.67 us
    psum x1 -> x0, waiting for transfers between devices: 277 us -> none  [shards(): mix = transform(lax.psum(gram, 'slab'))]
    unnamed x3 -> x0, waiting for transfers between devices: 268 us -> none
    pallas_call x2 -> x1, Pallas kernels: 34.3 us -> 88.9 us  [shards(): pl.pallas_call(body, name='cycle', out_shape=(jax.ShapeDtypeStruct((group...]
    all_gather x1 -> x0, blocking collectives: 44.8 us -> none  [shards(): predicted = lax.all_gather(mine, 'member', axis=0, tiled=True)]
    all_to_all x2 -> x0, starting transfers between devices: 27 us -> none  [the longest x1 14.7 us: shards(): lax.all_to_all(forecast, 'member', split_axis=1, concat_axis=0, tiled=True)]
    ppermute x4 -> x0, starting transfers between devices: 14.4 us -> none  [the longest x2 7.52 us: padded(): after = lax.ppermute(initial, axis, down)]
    all_to_all x2 -> x0, waiting for transfers between devices: 13.1 us -> none  [the longest x1 13.1 us: shards(): lax.all_to_all(analysed, 'member', split_axis=0, concat_axis=1, tiled=True)]
  transfers between devices with their start and end apart: 8 -> 0, of which waited for: 4 -> 0; matrix products, arithmetic and copies ran while one was open for 1% -> 0% of each run, Pallas kernels for 3% -> 0%
where the time goes in v2:
time: 95.2 us; the launch traced here: 94.9 us
  Pallas kernels  88.9 us (93%)
  local copies, waits for them, and re-layouts  5.41 us (6%)
    pallas_call x1, Pallas kernels, shards(): pl.pallas_call(body, name='cycle', out_shape=(jax.ShapeDtypeStruct((group...  88.9 us
    unnamed x6, local copies, waits for them, and re-layouts  2.19 us

profile of v2, /device:TPU:1, one launch (start us, length us, event | category | flops | bytes accessed | tf_op | source)
XLA Modules:
  0.0 94.9 jit_solution(15671511522399877521)
XLA Ops:
  0.6 0.0 copy-start
  0.6 1.7 %copy_bitcast_fusion = (f32[16,12,128]{2,1,0:T(8,128)}, f32[16,12,128]{2,1,0:T(8,128)}) fusion(f32[12,16,128]{2,1,0:T(8,128)} %param.9, f32[12,16,128]{2,1,0:T(8,128)} %param.8), kind=kLoop, calls=%fused_computation | loop fusion | bytes 393216 | tf_op jit(solution)/shard_map/transpose | solution.py:496
  2.3 0.0 copy-done
  2.3 0.3 reshape.10
  2.7 0.3 copy.16
  3.0 0.9 reshape.11.refs_4_
  3.9 88.9 %cycle.1 = (f32[16,12,128]{2,1,0:T(8,128)}, f32[8,192]{1,0:T(8,128)}) custom-call(f32[16,12,128]{2,1,0:T(8,128)} %get-tuple-element.11.refs_0_, f32[16,12,128]{2,1,0:T(8,128)} %get-tuple-element.10.refs_1_, f32[16,1,128]{2,1,0:T(1,128)} %bitcast.14, s32[16,128]{1,0:T(8,128)} %refs_3_.1, s32[2,4096]{1,0:T(2,128)} %reshape.11.refs_4_, s32[1,1024]{1,0:T(1,128)} %bitcast.15, ...), custom_call_target="tpu_custom_call" | custom-call | tf_op jit(solution)/shard_map/cycle/pallas_call | solution.py:445
  92.7 0.0 copy-start.1
  92.8 1.6 %copy.17 = f32[12,16,128]{2,1,0:T(8,128)} copy(f32[12,16,128]{2,0,1:T(8,128)} %bitcast.13) | data formatting | bytes 196608
  94.3 0.0 copy-done.1
  94.3 0.6 copy.21
Async XLA Ops:
  0.6 1.7 %copy-start = (s32[2,4096]{1,0:T(2,128)S(1)}, s32[2,4096]{1,0:T(2,128)}, u32[]{:S(2)}) copy-start(s32[2,4096]{1,0:T(2,128)} %param.12) | copy-start | bytes 98308
  92.7 1.6 %copy-start.1 = (f32[8,192]{1,0:T(8,128)S(1)}, f32[8,192]{1,0:T(8,128)}, u32[]{:S(2)}) copy-start(f32[8,192]{1,0:T(8,128)} %get-tuple-element.15) | copy-start | bytes 18436

commit v3 on v2

v3 whole, which is shorter than its diff:
```python
import math

import jax
import jax.numpy as jnp
from jax import lax
from jax.experimental import pallas as pl
from jax.experimental.pallas import tpu as pltpu
from jax.sharding import PartitionSpec as P

STEPS = 4
time_step = 0.15
pixel_span = 64.0
top_depth = 2.0
F32 = jnp.float32
BF16 = jnp.bfloat16
HIGHEST = lax.Precision.HIGHEST
MESH = pl.DeviceIdType.MESH
BLOCK = 256
LANES = 128
EARLY = 8
MIDDLE = 14
FIRST = 9


def split(value):
    high = value.astype(BF16)
    return high, (value - high.astype(F32)).astype(BF16)


def twice(value):
    return jnp.concatenate([value, value], axis=1)


def dot(a, b, dims):
    return lax.dot_general(a, b, (dims, ((), ())), precision=HIGHEST, preferred_element_type=F32)


def mm(a, b):
    return dot(a, b, ((1,), (0,)))


def mm_tn(a, b):
    return dot(a, b, ((0,), (0,)))


def mm_nt(a, b):
    return dot(a, b, ((1,), (1,)))


def inverse_factor(block):
    size = block.shape[0]
    wide = 2 * size
    count = size // 8
    sub = lax.broadcasted_iota(jnp.int32, (8, wide), 0)
    lane = lax.broadcasted_iota(jnp.int32, (8, wide), 1)

    def full(value):
        return jnp.broadcast_to(value, (8, wide))

    tiles = []
    for t in range(count):
        unit = jnp.where(lane == sub + (8 * t + size), 1.0, 0.0)
        tiles.append(jnp.concatenate([block[8 * t : 8 * t + 8], unit[:, size:]], axis=1))
    out = []
    for q in range(count):
        start = 8 * q
        cols = [
            [full(tiles[t][:, start + j : start + j + 1]) for t in range(q, count)] for j in range(8)
        ]
        lines = []
        top = tiles[q]
        pivots = None
        for k in range(8):
            mine = cols[k]
            pivot = full(mine[0][k : k + 1, :])
            pivots = pivot if k == 0 else jnp.where(sub == k, pivot, pivots)
            inv = 1.0 / pivot
            for j in range(k + 1, 8):
                ratio = full(mine[0][j : j + 1, :]) * inv
                cols[j] = [c - m * ratio for c, m in zip(cols[j], mine)]
            line = full(top[k : k + 1, :]) * inv
            lines.append(line)
            if k < 7:
                top = top - jnp.where(sub > k, mine[0], 0.0) * line
        out.append(top[:, size:] * lax.rsqrt(pivots)[:, size:])
        for t in range(q + 1, count):
            for k in range(8):
                tiles[t] = tiles[t] - cols[k][t - q] * lines[k]
    return jnp.concatenate(out, axis=0)


def transform(packed, rhs, members):
    size = members // 3
    row = lax.broadcasted_iota(jnp.int32, (members, 2 * size), 0)
    col = lax.broadcasted_iota(jnp.int32, (members, 2 * size), 1)
    gram = packed + jnp.where(row == col, members - 1.0, 0.0)
    corner = packed[0:size, size:] + jnp.where(row == col, members - 1.0, 0.0)[0:size, 0:size]
    l0 = inverse_factor(gram[0:size, 0:size])
    t0 = mm_nt(l0, gram[size:, 0:size])
    s1 = gram[size:, size:] - mm_tn(t0, t0[:, 0:size])
    z1 = -mm_tn(t0, l0)
    l1 = inverse_factor(s1[0:size])
    t1 = mm_nt(l1, s1[size:])
    l10 = mm(l1, z1[0:size])
    s2 = corner - mm_tn(t0[:, size:], t0[:, size:]) - mm_tn(t1, t1)
    z2 = jnp.concatenate([z1[size:] - mm_tn(t1, l10), -mm_tn(t1, l1)], axis=1)
    l2 = inverse_factor(s2)
    l20 = mm(l2, z2)
    zero = jnp.zeros((size, size), F32)
    inverse = jnp.concatenate(
        [
            jnp.concatenate([l0, zero, zero], axis=1),
            jnp.concatenate([l10, l1, zero], axis=1),
            jnp.concatenate([l20, l2], axis=1),
        ],
        axis=0,
    )
    reduced = jnp.sum(inverse * rhs, axis=1, keepdims=True)
    weights = jnp.sum(inverse * reduced, axis=0, keepdims=True)
    return weights + math.sqrt(members - 1.0) * inverse


def advance(head, perm, source, open_first, open_last, first_row, rows):
    mobility = perm * (1.0 + 0.5 * jnp.tanh(head))
    last = head.shape[0] - 1
    cols = head.shape[2]
    flux = 0.5 * (mobility[1:] + mobility[:-1]) * (head[1:] - head[:-1])
    parts = [flux[i : i + 1] for i in range(last)]
    near, far = STEPS - 1 - first_row, STEPS - 1 + rows - first_row
    parts[near] = parts[near] * open_first
    parts[far] = parts[far] * open_last
    flux = jnp.concatenate(parts, axis=0)
    inner = head[1:-1]
    own = mobility[1:-1]
    lane = lax.broadcasted_iota(jnp.int32, inner.shape, 2)
    along = 0.5 * (jnp.roll(own, -1, axis=2) + own) * (jnp.roll(inner, -1, axis=2) - inner)
    along = jnp.where(lane < cols - 1, along, 0.0)
    back = jnp.where(lane > 0, jnp.roll(along, 1, axis=2), 0.0)
    inflow = (flux[1:] - flux[:-1]) + (along - back)
    return inner + time_step * (inflow + source[1:-1])


def cycle_kernel(total_rows, *refs):
    head_ref, cond_ref, well_ref, lay_ref, pc_ref, oi_ref, ov_ref, os_ref = refs[:8]
    ret_ref, own_ref = refs[8:10]
    hx, cx, wx, fore, w_ref, h2_ref, vh_ref, khi, klo, ohi, olo, place, where = refs[10:23]
    po, ro, mine, ao, flat, part, rs, turned, got, gpart, gred, gall, pile, snd, back = refs[23:38]
    halo_s, halo_r, out_s, out_r, ro_s, ro_r, ao_s, ao_r = refs[38:46]
    g1_s, g1_r, rs_s, rs_r, g2_s, g2_r, tu_s, tu_r, rt_s, rt_r = refs[46:]

    slab, member = lax.axis_index("slab"), lax.axis_index("member")
    slabs, groups = lax.axis_size("slab"), lax.axis_size("member")
    rows, local, cols = head_ref.shape
    members = local * groups
    pixels = pc_ref.shape[1]
    observed = oi_ref.shape[1]
    blocks, obs_blocks = pixels // BLOCK, observed // BLOCK
    row_pitch, col_pitch = pixel_span / total_rows, pixel_span / cols
    volume = pixel_span * pixel_span / (total_rows * cols)

    def other(i, axis):
        me, n = (slab, slabs) if axis == "slab" else (member, groups)
        return lax.rem(me + i, n)

    def peers(axis, body):
        n = slabs if axis == "slab" else groups

        def step(i, carry):
            body(other(i, axis))
            return carry

        lax.fori_loop(1, n, step, 0)

    def copy(src, dst, ssem, rsem, axis, to):
        return pltpu.make_async_remote_copy(
            src_ref=src,
            dst_ref=dst,
            send_sem=ssem,
            recv_sem=rsem,
            device_id={axis: to},
            device_id_type=MESH,
        )

    class Exchange:
        def __init__(self, axis, src, dst, ssem, rsem):
            self.axis, self.src, self.dst, self.ssem, self.rsem = axis, src, dst, ssem, rsem
            self.me = slab if axis == "slab" else member

        def make(self, to, at):
            return copy(
                self.src(to), self.dst.at[at], self.ssem.at[to], self.rsem.at[at], self.axis, to
            )

        def start(self):
            peers(self.axis, lambda to: self.make(to, self.me).start())

        def arrive(self):
            peers(self.axis, lambda frm: self.make(frm, frm).wait_recv())

        def drain(self):
            peers(self.axis, lambda to: self.make(to, to).wait_send())

    def total_of(ref):
        value = ref[0]
        for n in range(1, ref.shape[0]):
            value += ref[n]
        return value

    send_fore = Exchange("member", lambda to: fore.at[to], pile, out_s, out_r)
    send_obs = Exchange("slab", lambda to: po.at[to], ro, ro_s, ro_r)
    send_mine = Exchange("member", lambda to: mine, ao, ao_s, ao_r)
    send_gram = Exchange("slab", lambda to: gpart.at[to], gred, g1_s, g1_r)
    send_part = Exchange("slab", lambda to: part.at[to], rs, rs_s, rs_r)
    send_sum = Exchange("slab", lambda to: gall.at[slab], gall, g2_s, g2_r)
    send_own = Exchange("member", lambda to: turned.at[to], got, tu_s, tu_r)
    send_back = Exchange("member", lambda to: snd.at[to], back, rt_s, rt_r)

    barrier = pltpu.get_barrier_semaphore()
    for axis in ("slab", "member"):
        peers(
            axis,
            lambda to: pl.semaphore_signal(barrier, inc=1, device_id={axis: to}, device_id_type=MESH),
        )

    depth = top_depth + lay_ref[...].astype(F32)
    depth = jnp.concatenate([depth, jnp.zeros((cols - rows, cols), F32)], axis=0).T
    for i in range(rows):
        column = depth[:, i : i + 1]
        h2_ref[i] = jnp.broadcast_to(column * column, (cols, LANES))
        vh_ref[i] = jnp.broadcast_to(volume * column, (cols, LANES))
    cell_y = (lax.broadcasted_iota(jnp.int32, (cols, BLOCK), 0).astype(F32) + 0.5) * col_pitch
    first = (slab * rows).astype(F32)

    def evaluate(coords_ref, high_ref, low_ref):
        def step(b, carry):
            at = pl.multiple_of(b * BLOCK, BLOCK)
            coords = coords_ref[0:2, pl.ds(at, BLOCK)].astype(F32)
            delta_y = cell_y - coords[1:2]
            dy2 = delta_y * delta_y
            for i in range(rows):
                delta_x = (first + (i + 0.5)) * row_pitch - coords[0:1]
                radius = (dy2 + delta_x * delta_x) + twice(h2_ref[i])
                inv = lax.rsqrt(radius)
                high, low = split(twice(vh_ref[i]) * (inv * inv * inv))
                high_ref[b, cols * i : cols * i + cols, :] = high
                low_ref[b, cols * i : cols * i + cols, :] = low
            return carry

        return step

    groups_of = pixels // LANES
    for c in range(2):
        for n in range(groups_of):
            place[groups_of * c + n : groups_of * c + n + 1, :] = pc_ref[
                c : c + 1, LANES * n : LANES * n + LANES
            ].astype(F32)
    index = oi_ref[...]
    own = LANES // groups
    chosen = (index // own) // slabs
    within = lax.rem(index // own, slabs) * LANES + chosen * own + lax.rem(index, own)
    high_part, low_part = within // LANES, lax.rem(within, LANES)
    line = lax.broadcasted_iota(jnp.int32, (groups_of, observed), 0)
    pick = jnp.where(line == high_part, 1.0, 0.0).astype(BF16)
    spot = lax.broadcasted_iota(jnp.int32, (LANES, observed), 0) == low_part
    for c in range(2):
        table = place[groups_of * c : groups_of * c + groups_of, :].astype(BF16)
        near = lax.dot_general(table, pick, (((0,), (0,)), ((), ())), preferred_element_type=F32)
        where[c : c + 1, :] = jnp.sum(jnp.where(spot, near, 0.0), axis=0, keepdims=True)
    lax.fori_loop(0, obs_blocks, evaluate(where, ohi, olo), 0)
    every = evaluate(pc_ref, khi, klo)
    lax.fori_loop(0, EARLY, every, 0)

    pl.semaphore_wait(barrier, slabs - 1 + groups - 1)

    up, down = other(1, "slab"), other(slabs - 1, "slab")
    halos = []
    for n, (src, dst) in enumerate(((head_ref, hx), (cond_ref, cx), (well_ref, wx))):
        for side, (frm, at, to) in enumerate(((rows - STEPS, 0, up), (0, rows + STEPS, down))):
            halos.append(
                copy(
                    src.at[pl.ds(frm, STEPS)],
                    dst.at[pl.ds(at, STEPS)],
                    halo_s.at[2 * n + side],
                    halo_r.at[2 * n + side],
                    "slab",
                    to,
                )
            )
    for item in halos:
        item.start()
    hx[STEPS : STEPS + rows] = head_ref[...]
    cx[STEPS : STEPS + rows] = cond_ref[...]
    wx[STEPS : STEPS + rows] = well_ref[...]
    lax.fori_loop(EARLY, MIDDLE, every, 0)
    width = observed // slabs
    inverse_var = 1.0 / (os_ref[...] * os_ref[...])
    first_line = lax.broadcasted_iota(jnp.int32, (8, observed), 0) == 0
    observations = jnp.where(first_line, inverse_var, ov_ref[...])
    observations = pltpu.roll(observations, lax.rem(observed - width * slab, observed), 1)
    inside = lax.broadcasted_iota(jnp.int32, (8, LANES), 1) < width
    observations = jnp.where(inside, observations[:, 0:LANES], 0.0)

    for item in halos:
        item.wait_recv()
    head, perm, source = hx[...], cx[...], wx[...]
    open_first = jnp.where(slab == 0, 0.0, 1.0)
    open_last = jnp.where(slab == slabs - 1, 0.0, 1.0)
    for k in range(STEPS):
        head = advance(head, perm, source, open_first, open_last, k, rows)
        perm, source = perm[1:-1], source[1:-1]
    fore[...] = head
    w_ref[...] = jnp.zeros_like(w_ref)
    for i in range(rows):
        high, low = split(head[i])
        w_ref[0:local, cols * i : cols * i + cols] = high
        w_ref[16 : 16 + local, cols * i : cols * i + cols] = low

    def product(high_ref, low_ref, b):
        total = jnp.dot(w_ref[...], high_ref[b], preferred_element_type=F32)
        return total + jnp.dot(w_ref[...], low_ref[b], preferred_element_type=F32)

    shares = LANES // width
    each = local // shares
    line = lax.broadcasted_iota(jnp.int32, (32, 32), 0)
    col = lax.broadcasted_iota(jnp.int32, (32, 32), 1)
    wanted = (line // 8) * each + lax.rem(line, 8)
    valid = lax.rem(line, 8) < each
    gather = jnp.where(valid & ((col == wanted) | (col == wanted + 16)), 1.0, 0.0)
    lane = lax.broadcasted_iota(jnp.int32, (8, LANES), 1) // width
    for b in range(obs_blocks):
        total = mm(gather, product(ohi, olo, b))
        for half in range(BLOCK // LANES):
            block = total[:, LANES * half : LANES * half + LANES]
            for u in range(shares):
                chunk = None
                for g in range(shares):
                    piece = pltpu.roll(block[8 * g : 8 * g + 8], (width * (g - u)) % LANES, 1)
                    chunk = piece if g == 0 else jnp.where(lane == g, piece, chunk)
                po[(b * (BLOCK // LANES) + half) * shares + u] = chunk[0:4]
    send_obs.start()
    send_fore.start()
    ro[slab] = po[slab]

    def whole(b, carry):
        total = product(khi, klo, b)
        total = total[0:16] + total[16:32]
        for half in range(BLOCK // LANES):
            part[b * (BLOCK // LANES) + half] = total[0:local, LANES * half : LANES * half + LANES]
        return carry

    lax.fori_loop(0, FIRST, whole, 0)
    send_obs.arrive()
    total = total_of(ro)
    mine[...] = total
    ao[member] = total
    send_mine.start()
    lax.fori_loop(MIDDLE, blocks, every, 0)
    lax.fori_loop(FIRST, blocks, whole, 0)
    send_obs.drain()
    send_mine.arrive()
    lane = lax.broadcasted_iota(jnp.int32, (4, LANES), 1)
    for n in range(groups):
        tile = ao[n]
        for g in range(shares):
            piece = tile if g == 0 else pltpu.roll(tile, LANES - width * g, 1)
            at = local * n + each * g
            flat[at : at + each, :] = jnp.where(lane < width, piece, 0.0)[0:each]
    predicted = flat[...]
    centre = jnp.sum(predicted, axis=0, keepdims=True) * (1.0 / members)
    anomaly = predicted - centre
    weight = observations[0:1]
    gram = mm_nt(anomaly, anomaly * weight)
    rhs = mm_nt(jnp.broadcast_to(weight * (observations[1:2] - centre), (8, LANES)), anomaly)
    size = members // 3
    top = jnp.concatenate([gram[0:size, 0:size], gram[2 * size :, 2 * size :]], axis=1)
    pieces = [top, gram[size:, 0 : 2 * size], rhs[:, 0:LANES]]
    pieces.append(jnp.concatenate([rhs[:, LANES:], jnp.zeros((8, 2 * LANES - members), F32)], axis=1))
    height = gpart.shape[1]
    pieces.append(jnp.zeros((slabs * height - members - 16, LANES), F32))
    gpart[...] = jnp.concatenate(pieces, axis=0).reshape(slabs, height, LANES)
    send_gram.start()
    send_part.start()
    rs[slab] = part[slab]
    gred[slab] = gpart[slab]
    send_mine.drain()
    send_gram.arrive()
    gall[slab] = total_of(gred)
    send_sum.start()
    send_gram.drain()
    send_fore.arrive()
    pile[member] = fore[member]
    for n in range(groups):
        flat[local * n : local * n + local, :] = pile[n]
    spread = flat[...]
    centre = jnp.sum(spread, axis=0, keepdims=True) * (1.0 / members)
    spread = spread - centre
    send_part.arrive()
    total = jnp.concatenate([total_of(rs), jnp.zeros((LANES - local, LANES), F32)], axis=0)
    turned[...] = total.T.reshape(groups, own, LANES)
    send_sum.arrive()
    send_own.start()
    got[member] = turned[member]
    packed = gall[...].reshape(slabs * height, LANES)
    rhs = jnp.concatenate(
        [packed[members : members + 1], packed[members + 8 : members + 9]], axis=1
    )[:, 0:members]
    mix = transform(packed[0:members], rhs, members)
    flat[...] = centre + mm(mix, spread)
    for n in range(groups):
        snd[n] = flat[local * n : local * n + local, :]
    send_back.start()
    back[member] = snd[member]
    send_own.arrive()
    total = jnp.zeros((own, 2 * LANES), F32)
    for n in range(groups):
        tile = jnp.concatenate([got[n], jnp.zeros((own, LANES), F32)], axis=1)
        total += tile if n == 0 else pltpu.roll(tile, local * n, 1)
    own_ref[...] = total[:, 0:members]
    for item in halos:
        item.wait_send()
    send_fore.drain()
    send_part.drain()
    send_sum.drain()
    send_own.drain()
    send_back.arrive()
    ret_ref[...] = back[...]
    send_back.drain()


def shards(
    fluid_head_start,
    conductivity_matrix,
    well_rates,
    cell_layer,
    pixel_coords,
    obs_index,
    obs_value,
    obs_sigma,
):
    local, rows, cols = fluid_head_start.shape
    groups = lax.axis_size("member")
    slabs = lax.axis_size("slab")
    members = local * groups
    pixels = pixel_coords.shape[1]
    observed = obs_index.shape[0]
    own = pixels // (groups * slabs)
    height = 256 // slabs
    coords = pixel_coords.reshape(-1, groups, slabs, own).transpose(0, 2, 1, 3).reshape(-1, pixels)
    place = pl.BlockSpec(memory_space=pltpu.VMEM)
    tall = rows + 2 * STEPS

    def f32(*shape):
        return pltpu.VMEM(shape, F32)

    def bf16(*shape):
        return pltpu.VMEM(shape, BF16)

    def pair(n):
        return [pltpu.SemaphoreType.DMA((n,))] * 2

    body = lambda *refs: cycle_kernel(rows * slabs, *refs)
    returned, own_part = pl.pallas_call(
        body,
        name="cycle",
        out_shape=(
            jax.ShapeDtypeStruct((groups, local, cols), F32),
            jax.ShapeDtypeStruct((own, members), F32),
        ),
        in_specs=[place] * 8,
        out_specs=(place, place),
        scratch_shapes=[
            f32(tall, local, cols),
            f32(tall, local, cols),
            f32(tall, 1, cols),
            f32(rows, local, cols),
            bf16(32, rows * cols),
            f32(rows, cols, LANES),
            f32(rows, cols, LANES),
            bf16(pixels // BLOCK, rows * cols, BLOCK),
            bf16(pixels // BLOCK, rows * cols, BLOCK),
            bf16(observed // BLOCK, rows * cols, BLOCK),
            bf16(observed // BLOCK, rows * cols, BLOCK),
            f32(2 * pixels // LANES, LANES),
            f32(8, observed),
            f32(slabs, 4, LANES),
            f32(slabs, 4, LANES),
            f32(4, LANES),
            f32(groups, 4, LANES),
            f32(members, LANES),
            f32(slabs, local, LANES),
            f32(slabs, local, LANES),
            f32(groups, own, LANES),
            f32(groups, own, LANES),
            f32(slabs, height, LANES),
            f32(slabs, height, LANES),
            f32(slabs, height, LANES),
            f32(groups, local, cols),
            f32(groups, local, cols),
            f32(groups, local, cols),
            *pair(6),
            *pair(groups),
            *pair(slabs),
            *pair(groups),
            *pair(slabs),
            *pair(slabs),
            *pair(slabs),
            *pair(groups),
            *pair(groups),
        ],
        compiler_params=pltpu.CompilerParams(
            collective_id=0, has_side_effects=True, vmem_limit_bytes=60 * 1024 * 1024
        ),
    )(
        fluid_head_start.transpose(1, 0, 2),
        conductivity_matrix.transpose(1, 0, 2),
        well_rates[:, None, :],
        cell_layer,
        coords,
        obs_index[None],
        obs_value[None],
        obs_sigma[None],
    )
    return (returned.transpose(1, 0, 2), own_part)


def solution(mesh):
    return jax.shard_map(
        shards,
        mesh=mesh,
        in_specs=(
            P("member", "slab", None),
            P("member", "slab", None),
            P("slab", None),
            P("slab", None),
            P(),
            P(),
            P(),
            P(),
        ),
        out_specs=(P("member", "slab", None), P(("member", "slab"), None)),
        check_vma=False,
    )
```

time: 95.2 us -> 84.2 us (0.88); the launches traced: 94.9 us -> 82.7 us
  Pallas kernels: 88.9 us -> 76.7 us
    pallas_call x1, Pallas kernels: 88.9 us -> 76.7 us  [shards(): pl.pallas_call(body, name='cycle', out_shape=(jax.ShapeDtypeStruct((group...]
where the time goes in v3:
time: 84.2 us; the launch traced here: 82.7 us
  Pallas kernels  76.7 us (91%)
  local copies, waits for them, and re-layouts  5.41 us (6%)
    pallas_call x1, Pallas kernels, shards(): pl.pallas_call(body, name='cycle', out_shape=(jax.ShapeDtypeStruct((group...  76.7 us
    unnamed x6, local copies, waits for them, and re-layouts  2.19 us
    transpose x1, local copies, waits for them, and re-layouts, shards(): conductivity_matrix.transpose(1, 0, 2)  1.7 us

profile of v3, /device:TPU:1, one launch (start us, length us, event | category | flops | bytes accessed | tf_op | source)
XLA Modules:
  0.0 82.7 jit_solution(16122804769256693064)
XLA Ops:
  0.6 0.0 copy-start
  0.6 1.7 %copy_bitcast_fusion = (f32[16,12,128]{2,1,0:T(8,128)}, f32[16,12,128]{2,1,0:T(8,128)}) fusion(f32[12,16,128]{2,1,0:T(8,128)} %param.9, f32[12,16,128]{2,1,0:T(8,128)} %param.8), kind=kLoop, calls=%fused_computation | loop fusion | bytes 393216 | tf_op jit(solution)/shard_map/transpose | solution.py:515
  2.3 0.0 copy-done
  2.3 0.3 reshape.10
  2.7 0.3 copy.16
  3.0 0.9 %reshape.11.refs_4_ = s32[2,4096]{1,0:T(2,128)} reshape(s32[2,32,16,8]{3,2,1,0:T(8,128)S(1)} %copy.16) | data formatting | bytes 65536 | tf_op jit(solution)/shard_map/reshape | solution.py:448
  3.9 76.7 %cycle.1 = (f32[16,12,128]{2,1,0:T(8,128)}, f32[8,192]{1,0:T(8,128)}) custom-call(f32[16,12,128]{2,1,0:T(8,128)} %get-tuple-element.11.refs_0_, f32[16,12,128]{2,1,0:T(8,128)} %get-tuple-element.10.refs_1_, f32[16,1,128]{2,1,0:T(1,128)} %bitcast.14, s32[16,128]{1,0:T(8,128)} %refs_3_.1, s32[2,4096]{1,0:T(2,128)} %reshape.11.refs_4_, s32[1,1024]{1,0:T(1,128)} %bitcast.15, ...), custom_call_target="tpu_custom_call" | custom-call | tf_op jit(solution)/shard_map/cycle/pallas_call | solution.py:462
  80.6 0.0 copy-start.1
  80.6 1.6 %copy.17 = f32[12,16,128]{2,1,0:T(8,128)} copy(f32[12,16,128]{2,0,1:T(8,128)} %bitcast.13) | data formatting | bytes 196608
  82.1 0.0 copy-done.1
  82.1 0.6 copy.21
Async XLA Ops:
  0.6 1.7 %copy-start = (s32[2,4096]{1,0:T(2,128)S(1)}, s32[2,4096]{1,0:T(2,128)}, u32[]{:S(2)}) copy-start(s32[2,4096]{1,0:T(2,128)} %param.12) | copy-start | bytes 98308
  80.6 1.6 %copy-start.1 = (f32[8,192]{1,0:T(8,128)S(1)}, f32[8,192]{1,0:T(8,128)}, u32[]{:S(2)}) copy-start(f32[8,192]{1,0:T(8,128)} %get-tuple-element.15) | copy-start | bytes 18436

commit v4 on v3

--- a/solution.py
+++ b/solution.py
@@ -17,8 +17,9 @@
 MESH = pl.DeviceIdType.MESH
 BLOCK = 256
 LANES = 128
-EARLY = 8
-MIDDLE = 14
+EARLY = 3
+MIDDLE = 9
+LATE = 11
 FIRST = 9
 
 
@@ -144,13 +145,13 @@
     head_ref, cond_ref, well_ref, lay_ref, pc_ref, oi_ref, ov_ref, os_ref = refs[:8]
     ret_ref, own_ref = refs[8:10]
     hx, cx, wx, fore, w_ref, h2_ref, vh_ref, khi, klo, ohi, olo, place, where = refs[10:23]
-    po, ro, mine, ao, flat, part, rs, turned, got, gpart, gred, gall, pile, snd, back = refs[23:38]
-    halo_s, halo_r, out_s, out_r, ro_s, ro_r, ao_s, ao_r = refs[38:46]
-    g1_s, g1_r, rs_s, rs_r, g2_s, g2_r, tu_s, tu_r, rt_s, rt_r = refs[46:]
+    pcs, po, ro, mine, ao, flat, part, rs, turned, got, gpart, gred, gall, pile, snd, back = refs[23:39]
+    halo_s, halo_r, out_s, out_r, ro_s, ro_r, ao_s, ao_r = refs[39:47]
+    g1_s, g1_r, rs_s, rs_r, g2_s, g2_r, tu_s, tu_r, rt_s, rt_r = refs[47:]
 
     slab, member = lax.axis_index("slab"), lax.axis_index("member")
     slabs, groups = lax.axis_size("slab"), lax.axis_size("member")
-    rows, local, cols = head_ref.shape
+    local, rows, cols = head_ref.shape
     members = local * groups
     pixels = pc_ref.shape[1]
     observed = oi_ref.shape[1]
@@ -186,19 +187,23 @@
             self.axis, self.src, self.dst, self.ssem, self.rsem = axis, src, dst, ssem, rsem
             self.me = slab if axis == "slab" else member
 
-        def make(self, to, at):
-            return copy(
-                self.src(to), self.dst.at[at], self.ssem.at[to], self.rsem.at[at], self.axis, to
-            )
-
         def start(self):
-            peers(self.axis, lambda to: self.make(to, self.me).start())
+            def one(to):
+                copy(
+                    self.src(to), self.dst.at[self.me], self.ssem, self.rsem, self.axis, to
+                ).start()
+
+            peers(self.axis, one)
+
+        def every(self):
+            part = self.dst.at[pl.ds(0, self.dst.shape[0] - 1)]
+            return copy(part, part, self.ssem, self.rsem, self.axis, other(1, self.axis))
 
         def arrive(self):
-            peers(self.axis, lambda frm: self.make(frm, frm).wait_recv())
+            self.every().wait_recv()
 
         def drain(self):
-            peers(self.axis, lambda to: self.make(to, to).wait_send())
+            self.every().wait_send()
 
     def total_of(ref):
         value = ref[0]
@@ -222,6 +227,10 @@
             lambda to: pl.semaphore_signal(barrier, inc=1, device_id={axis: to}, device_id_type=MESH),
         )
 
+    for i in range(rows):
+        hx[STEPS + i] = head_ref[:, i, :]
+        cx[STEPS + i] = cond_ref[:, i, :]
+        wx[STEPS + i] = well_ref[i : i + 1, :]
     depth = top_depth + lay_ref[...].astype(F32)
     depth = jnp.concatenate([depth, jnp.zeros((cols - rows, cols), F32)], axis=0).T
     for i in range(rows):
@@ -254,32 +263,46 @@
             place[groups_of * c + n : groups_of * c + n + 1, :] = pc_ref[
                 c : c + 1, LANES * n : LANES * n + LANES
             ].astype(F32)
-    index = oi_ref[...]
     own = LANES // groups
-    chosen = (index // own) // slabs
-    within = lax.rem(index // own, slabs) * LANES + chosen * own + lax.rem(index, own)
-    high_part, low_part = within // LANES, lax.rem(within, LANES)
+    near = slabs * own // LANES
+    line = lax.broadcasted_iota(jnp.int32, (groups, LANES), 0)
+    lane = lax.broadcasted_iota(jnp.int32, (groups, LANES), 1)
+    widen = jnp.where(lane // own == line, 1.0, 0.0).astype(BF16)
+    line = lax.broadcasted_iota(jnp.int32, (LANES, LANES), 0)
+    lane = lax.broadcasted_iota(jnp.int32, (LANES, LANES), 1)
+    same = lax.rem(line, own) == lax.rem(lane, own)
+    for c in range(2):
+        for h in range(near):
+            table = place[pl.ds(groups_of * c + h, groups, stride=near), :].astype(BF16)
+            wide = lax.dot_general(
+                table, widen, (((0,), (0,)), ((), ())), preferred_element_type=F32
+            )
+            wide = jnp.sum(jnp.where(same, wide, 0.0).reshape(LANES // own, own, LANES), axis=1)
+            for n in range(LANES // own):
+                at = (h * (LANES // own) + n) * LANES
+                pcs[c : c + 1, at : at + LANES] = wide[n : n + 1]
+    high_part, low_part = oi_ref[...] // LANES, lax.rem(oi_ref[...], LANES)
     line = lax.broadcasted_iota(jnp.int32, (groups_of, observed), 0)
     pick = jnp.where(line == high_part, 1.0, 0.0).astype(BF16)
     spot = lax.broadcasted_iota(jnp.int32, (LANES, observed), 0) == low_part
     for c in range(2):
         table = place[groups_of * c : groups_of * c + groups_of, :].astype(BF16)
-        near = lax.dot_general(table, pick, (((0,), (0,)), ((), ())), preferred_element_type=F32)
-        where[c : c + 1, :] = jnp.sum(jnp.where(spot, near, 0.0), axis=0, keepdims=True)
+        found = lax.dot_general(table, pick, (((0,), (0,)), ((), ())), preferred_element_type=F32)
+        where[c : c + 1, :] = jnp.sum(jnp.where(spot, found, 0.0), axis=0, keepdims=True)
     lax.fori_loop(0, obs_blocks, evaluate(where, ohi, olo), 0)
-    every = evaluate(pc_ref, khi, klo)
+    every = evaluate(pcs, khi, klo)
     lax.fori_loop(0, EARLY, every, 0)
 
     pl.semaphore_wait(barrier, slabs - 1 + groups - 1)
 
     up, down = other(1, "slab"), other(slabs - 1, "slab")
     halos = []
-    for n, (src, dst) in enumerate(((head_ref, hx), (cond_ref, cx), (well_ref, wx))):
-        for side, (frm, at, to) in enumerate(((rows - STEPS, 0, up), (0, rows + STEPS, down))):
+    for n, grown in enumerate((hx, cx, wx)):
+        for side, (frm, at, to) in enumerate(((rows, 0, up), (STEPS, rows + STEPS, down))):
             halos.append(
                 copy(
-                    src.at[pl.ds(frm, STEPS)],
-                    dst.at[pl.ds(at, STEPS)],
+                    grown.at[pl.ds(frm, STEPS)],
+                    grown.at[pl.ds(at, STEPS)],
                     halo_s.at[2 * n + side],
                     halo_r.at[2 * n + side],
                     "slab",
@@ -288,9 +311,6 @@
             )
     for item in halos:
         item.start()
-    hx[STEPS : STEPS + rows] = head_ref[...]
-    cx[STEPS : STEPS + rows] = cond_ref[...]
-    wx[STEPS : STEPS + rows] = well_ref[...]
     lax.fori_loop(EARLY, MIDDLE, every, 0)
     width = observed // slabs
     inverse_var = 1.0 / (os_ref[...] * os_ref[...])
@@ -349,13 +369,15 @@
         return carry
 
     lax.fori_loop(0, FIRST, whole, 0)
+    lax.fori_loop(MIDDLE, LATE, every, 0)
     send_obs.arrive()
     total = total_of(ro)
     mine[...] = total
     ao[member] = total
     send_mine.start()
-    lax.fori_loop(MIDDLE, blocks, every, 0)
+    lax.fori_loop(LATE, blocks, every, 0)
     lax.fori_loop(FIRST, blocks, whole, 0)
+    send_part.start()
     send_obs.drain()
     send_mine.arrive()
     lane = lax.broadcasted_iota(jnp.int32, (4, LANES), 1)
@@ -379,7 +401,6 @@
     pieces.append(jnp.zeros((slabs * height - members - 16, LANES), F32))
     gpart[...] = jnp.concatenate(pieces, axis=0).reshape(slabs, height, LANES)
     send_gram.start()
-    send_part.start()
     rs[slab] = part[slab]
     gred[slab] = gpart[slab]
     send_mine.drain()
@@ -423,7 +444,8 @@
     send_sum.drain()
     send_own.drain()
     send_back.arrive()
-    ret_ref[...] = back[...]
+    for i in range(rows):
+        ret_ref[:, i, :] = back[i]
     send_back.drain()
 
 
@@ -445,7 +467,6 @@
     observed = obs_index.shape[0]
     own = pixels // (groups * slabs)
     height = 256 // slabs
-    coords = pixel_coords.reshape(-1, groups, slabs, own).transpose(0, 2, 1, 3).reshape(-1, pixels)
     place = pl.BlockSpec(memory_space=pltpu.VMEM)
     tall = rows + 2 * STEPS
 
@@ -455,15 +476,15 @@
     def bf16(*shape):
         return pltpu.VMEM(shape, BF16)
 
-    def pair(n):
-        return [pltpu.SemaphoreType.DMA((n,))] * 2
+    def pair(shape):
+        return [pltpu.SemaphoreType.DMA(shape)] * 2
 
     body = lambda *refs: cycle_kernel(rows * slabs, *refs)
     returned, own_part = pl.pallas_call(
         body,
         name="cycle",
         out_shape=(
-            jax.ShapeDtypeStruct((groups, local, cols), F32),
+            jax.ShapeDtypeStruct((local, rows, cols), F32),
             jax.ShapeDtypeStruct((own, members), F32),
         ),
         in_specs=[place] * 8,
@@ -482,6 +503,7 @@
             bf16(observed // BLOCK, rows * cols, BLOCK),
             f32(2 * pixels // LANES, LANES),
             f32(8, observed),
+            f32(2, pixels),
             f32(slabs, 4, LANES),
             f32(slabs, 4, LANES),
             f32(4, LANES),
@@ -497,30 +519,23 @@
             f32(groups, local, cols),
             f32(groups, local, cols),
             f32(groups, local, cols),
-            *pair(6),
-            *pair(groups),
-            *pair(slabs),
-            *pair(groups),
-            *pair(slabs),
-            *pair(slabs),
-            *pair(slabs),
-            *pair(groups),
-            *pair(groups),
+            *pair((6,)),
+            *(pair(()) * 8),
         ],
         compiler_params=pltpu.CompilerParams(
             collective_id=0, has_side_effects=True, vmem_limit_bytes=60 * 1024 * 1024
         ),
     )(
-        fluid_head_start.transpose(1, 0, 2),
-        conductivity_matrix.transpose(1, 0, 2),
-        well_rates[:, None, :],
+        fluid_head_start,
+        conductivity_matrix,
+        well_rates,
         cell_layer,
-        coords,
+        pixel_coords,
         obs_index[None],
         obs_value[None],
         obs_sigma[None],
     )
-    return (returned.transpose(1, 0, 2), own_part)
+    return (returned, own_part)
 
 
 def solution(mesh):

time: 84.2 us -> 76.8 us (0.912)
  Pallas kernels: 76.7 us -> 72.7 us
  local copies, waits for them, and re-layouts: 5.41 us -> 2.15 us
    pallas_call x1, Pallas kernels: 76.7 us -> 72.7 us  [shards(): pl.pallas_call(body, name='cycle', out_shape=(jax.ShapeDtypeStruct((local...]
    transpose x2 -> x0, local copies, waits for them, and re-layouts: 2.01 us -> none  [the longest x1 1.7 us: shards(): conductivity_matrix.transpose(1, 0, 2)]
    reshape x2 -> x0, local copies, waits for them, and re-layouts: 1.2 us -> none  [shards(): pixel_coords.reshape(-1, groups, slabs, own).transpose(0, 2, 1, 3)]
    unnamed x6 -> x4, local copies, waits for them, and re-layouts: 2.19 us -> 2.15 us
where the time goes in v4:
time: 76.8 us; the launch traced here: 75.5 us
  Pallas kernels  72.7 us (95%)
  local copies, waits for them, and re-layouts  2.15 us (3%)
    pallas_call x1, Pallas kernels, shards(): pl.pallas_call(body, name='cycle', out_shape=(jax.ShapeDtypeStruct((local...  72.7 us
    unnamed x4, local copies, waits for them, and re-layouts  2.15 us

profile of v4, /device:TPU:1, one launch (start us, length us, event | category | flops | bytes accessed | tf_op | source)
XLA Modules:
  0.0 75.5 jit_solution(13656417686500444423)
XLA Ops:
  0.6 72.7 %cycle.1 = (f32[12,16,128]{2,1,0:T(8,128)}, f32[8,192]{1,0:T(8,128)}) custom-call(f32[12,16,128]{2,1,0:T(8,128)} %refs_0_.1, f32[12,16,128]{2,1,0:T(8,128)} %refs_1_.1, f32[16,128]{1,0:T(8,128)} %refs_2_.1, s32[16,128]{1,0:T(8,128)} %refs_3_.1, s32[2,4096]{1,0:T(2,128)} %refs_4_.1, s32[1,1024]{1,0:T(1,128)} %bitcast.3, f32[1,1024]{1,0:T(1,128)} %bitcast.4, ...), custom_call_target="tpu_custom_call" | custom-call | tf_op jit(solution)/shard_map/cycle/pallas_call | solution.py:483
  73.4 0.0 copy-start
  73.4 1.5 %copy.12 = f32[12,16,128]{2,1,0:T(8,128)} copy(f32[12,16,128]{2,1,0:T(8,128)} %get-tuple-element.4) | data formatting | bytes 196608
  74.9 0.0 copy-done
  74.9 0.6 copy.13
Async XLA Ops:
  73.4 1.6 %copy-start = (f32[8,192]{1,0:T(8,128)S(1)}, f32[8,192]{1,0:T(8,128)}, u32[]{:S(2)}) copy-start(f32[8,192]{1,0:T(8,128)} %get-tuple-element.5) | copy-start | bytes 18436

commit v5 on v4

--- a/solution.py
+++ b/solution.py
@@ -20,7 +20,8 @@
 EARLY = 3
 MIDDLE = 9
 LATE = 11
-FIRST = 9
+FIRST = 7
+DEEP = 4
 
 
 def split(value):
@@ -71,18 +72,29 @@
         lines = []
         top = tiles[q]
         pivots = None
-        for k in range(8):
-            mine = cols[k]
-            pivot = full(mine[0][k : k + 1, :])
-            pivots = pivot if k == 0 else jnp.where(sub == k, pivot, pivots)
-            inv = 1.0 / pivot
-            for j in range(k + 1, 8):
-                ratio = full(mine[0][j : j + 1, :]) * inv
-                cols[j] = [c - m * ratio for c, m in zip(cols[j], mine)]
-            line = full(top[k : k + 1, :]) * inv
-            lines.append(line)
-            if k < 7:
-                top = top - jnp.where(sub > k, mine[0], 0.0) * line
+        for k in range(0, 8, 2):
+            left, right = cols[k], cols[k + 1]
+            a = full(left[0][k : k + 1, :])
+            b = full(left[0][k + 1 : k + 2, :])
+            d = full(right[0][k + 1 : k + 2, :])
+            det = a * d - b * b
+            inv = 1.0 / det
+            for j in range(k + 2, 8):
+                u = full(left[0][j : j + 1, :])
+                v = full(right[0][j : j + 1, :])
+                p = (d * u - b * v) * inv
+                r = (a * v - b * u) * inv
+                cols[j] = [c - (x * p + y * r) for c, x, y in zip(cols[j], left, right)]
+            u = full(top[k : k + 1, :])
+            v = full(top[k + 1 : k + 2, :])
+            p = (d * u - b * v) * inv
+            r = (a * v - b * u) * inv
+            lines += [p, r]
+            ratio = 1.0 / a
+            first = jnp.where(sub == k, a, det * ratio)
+            pivots = first if k == 0 else jnp.where(sub >= k, first, pivots)
+            step = left[0] * p + right[0] * r
+            top = top - jnp.where(sub > k + 1, step, jnp.where(sub == k + 1, (b * ratio) * u, 0.0))
         out.append(top[:, size:] * lax.rsqrt(pivots)[:, size:])
         for t in range(q + 1, count):
             for k in range(8):
@@ -142,7 +154,9 @@
 
 
 def cycle_kernel(total_rows, *refs):
-    head_ref, cond_ref, well_ref, lay_ref, pc_ref, oi_ref, ov_ref, os_ref = refs[:8]
+    arguments, staged, staged_s = refs[:8], refs[-9:-1], refs[-1]
+    refs = refs[:-9]
+    head_ref, cond_ref, well_ref, lay_ref, pc_ref, oi_ref, ov_ref, os_ref = staged
     ret_ref, own_ref = refs[8:10]
     hx, cx, wx, fore, w_ref, h2_ref, vh_ref, khi, klo, ohi, olo, place, where = refs[10:23]
     pcs, po, ro, mine, ao, flat, part, rs, turned, got, gpart, gred, gall, pile, snd, back = refs[23:39]
@@ -172,6 +186,23 @@
 
         lax.fori_loop(1, n, step, 0)
 
+    def far_first(axis, body):
+        inner = groups // DEEP if axis == "member" else slabs // DEEP
+        for dz in (2, 1, 3, 0):
+
+            def step(i, carry):
+                if axis == "member":
+                    to = lax.rem(member // DEEP + i, inner) * DEEP
+                    to = to + lax.rem(member + dz, DEEP)
+                else:
+                    wide = 2 * DEEP
+                    to = lax.rem(slab // wide + i // 2, slabs // wide) * wide
+                    to = to + lax.rem(slab // 2 + dz, DEEP) * 2 + lax.rem(slab + i, 2)
+                body(to)
+                return carry
+
+            lax.fori_loop(1 if dz == 0 else 0, inner, step, 0)
+
     def copy(src, dst, ssem, rsem, axis, to):
         return pltpu.make_async_remote_copy(
             src_ref=src,
@@ -187,13 +218,11 @@
             self.axis, self.src, self.dst, self.ssem, self.rsem = axis, src, dst, ssem, rsem
             self.me = slab if axis == "slab" else member
 
+        def one(self, to):
+            copy(self.src(to), self.dst.at[self.me], self.ssem, self.rsem, self.axis, to).start()
+
         def start(self):
-            def one(to):
-                copy(
-                    self.src(to), self.dst.at[self.me], self.ssem, self.rsem, self.axis, to
-                ).start()
-
-            peers(self.axis, one)
+            far_first(self.axis, self.one)
 
         def every(self):
             part = self.dst.at[pl.ds(0, self.dst.shape[0] - 1)]
@@ -220,6 +249,12 @@
     send_own = Exchange("member", lambda to: turned.at[to], got, tu_s, tu_r)
     send_back = Exchange("member", lambda to: snd.at[to], back, rt_s, rt_r)
 
+    loads = [
+        pltpu.make_async_copy(src, dst, staged_s.at[n])
+        for n, (src, dst) in enumerate(zip(arguments, staged))
+    ]
+    for item in loads:
+        item.start()
     barrier = pltpu.get_barrier_semaphore()
     for axis in ("slab", "member"):
         peers(
@@ -227,6 +262,8 @@
             lambda to: pl.semaphore_signal(barrier, inc=1, device_id={axis: to}, device_id_type=MESH),
         )
 
+    for item in loads:
+        item.wait()
     for i in range(rows):
         hx[STEPS + i] = head_ref[:, i, :]
         cx[STEPS + i] = cond_ref[:, i, :]
@@ -241,7 +278,8 @@
     first = (slab * rows).astype(F32)
 
     def evaluate(coords_ref, high_ref, low_ref):
-        def step(b, carry):
+        def step(n, carry):
+            b = lax.rem(n + slab // 2, coords_ref.shape[1] // BLOCK)
             at = pl.multiple_of(b * BLOCK, BLOCK)
             coords = coords_ref[0:2, pl.ds(at, BLOCK)].astype(F32)
             delta_y = cell_y - coords[1:2]
@@ -347,7 +385,8 @@
     valid = lax.rem(line, 8) < each
     gather = jnp.where(valid & ((col == wanted) | (col == wanted + 16)), 1.0, 0.0)
     lane = lax.broadcasted_iota(jnp.int32, (8, LANES), 1) // width
-    for b in range(obs_blocks):
+    for n in range(obs_blocks):
+        b = lax.rem(n + slab // (slabs // obs_blocks), obs_blocks)
         total = mm(gather, product(ohi, olo, b))
         for half in range(BLOCK // LANES):
             block = total[:, LANES * half : LANES * half + LANES]
@@ -357,18 +396,41 @@
                     piece = pltpu.roll(block[8 * g : 8 * g + 8], (width * (g - u)) % LANES, 1)
                     chunk = piece if g == 0 else jnp.where(lane == g, piece, chunk)
                 po[(b * (BLOCK // LANES) + half) * shares + u] = chunk[0:4]
-    send_obs.start()
+        count = slabs // obs_blocks
+
+        def send(i, carry):
+            to = b * count + lax.rem(i + slab, count)
+
+            @pl.when(to != slab)
+            def _():
+                send_obs.one(to)
+
+            return carry
+
+        lax.fori_loop(0, count, send, 0)
     send_fore.start()
     ro[slab] = po[slab]
 
-    def whole(b, carry):
+    def whole(n, carry):
+        b = lax.rem(n + slab // 2, blocks)
         total = product(khi, klo, b)
         total = total[0:16] + total[16:32]
         for half in range(BLOCK // LANES):
             part[b * (BLOCK // LANES) + half] = total[0:local, LANES * half : LANES * half + LANES]
         return carry
 
+    def send_parts(n, carry):
+        to = lax.rem(n + (slab // 2) * (BLOCK // LANES), slabs)
+
+        @pl.when(to != slab)
+        def _():
+            send_part.one(to)
+
+        return carry
+
+    burst = FIRST * (BLOCK // LANES)
     lax.fori_loop(0, FIRST, whole, 0)
+    lax.fori_loop(0, burst, send_parts, 0)
     lax.fori_loop(MIDDLE, LATE, every, 0)
     send_obs.arrive()
     total = total_of(ro)
@@ -377,7 +439,7 @@
     send_mine.start()
     lax.fori_loop(LATE, blocks, every, 0)
     lax.fori_loop(FIRST, blocks, whole, 0)
-    send_part.start()
+    lax.fori_loop(burst, slabs, send_parts, 0)
     send_obs.drain()
     send_mine.arrive()
     lane = lax.broadcasted_iota(jnp.int32, (4, LANES), 1)
@@ -480,6 +542,16 @@
         return [pltpu.SemaphoreType.DMA(shape)] * 2
 
     body = lambda *refs: cycle_kernel(rows * slabs, *refs)
+    arguments = (
+        fluid_head_start,
+        conductivity_matrix,
+        well_rates,
+        cell_layer,
+        pixel_coords,
+        obs_index[None],
+        obs_value[None],
+        obs_sigma[None],
+    )
     returned, own_part = pl.pallas_call(
         body,
         name="cycle",
@@ -487,7 +559,7 @@
             jax.ShapeDtypeStruct((local, rows, cols), F32),
             jax.ShapeDtypeStruct((own, members), F32),
         ),
-        in_specs=[place] * 8,
+        in_specs=[pl.BlockSpec(memory_space=pltpu.HBM)] * 8,
         out_specs=(place, place),
         scratch_shapes=[
             f32(tall, local, cols),
@@ -521,20 +593,13 @@
             f32(groups, local, cols),
             *pair((6,)),
             *(pair(()) * 8),
+            *(pltpu.VMEM(value.shape, value.dtype) for value in arguments),
+            pltpu.SemaphoreType.DMA((len(arguments),)),
         ],
         compiler_params=pltpu.CompilerParams(
-            collective_id=0, has_side_effects=True, vmem_limit_bytes=60 * 1024 * 1024
+            collective_id=0, has_side_effects=True, vmem_limit_bytes=52 * 1024 * 1024
         ),
-    )(
-        fluid_head_start,
-        conductivity_matrix,
-        well_rates,
-        cell_layer,
-        pixel_coords,
-        obs_index[None],
-        obs_value[None],
-        obs_sigma[None],
-    )
+    )(*(pltpu.with_memory_space_constraint(value, pltpu.HBM) for value in arguments))
     return (returned, own_part)
 
 

time: 76.8 us -> 73.1 us (0.952)
  Pallas kernels: 72.7 us -> 70.4 us
  local copies, waits for them, and re-layouts: 2.15 us -> 1.24 us
    pallas_call x1, Pallas kernels: 72.7 us -> 70.4 us  [shards(): pl.pallas_call(body, name='cycle', out_shape=(jax.ShapeDtypeStruct((local...]
    unnamed x4 -> x2, local copies, waits for them, and re-layouts: 2.15 us -> 1.24 us
where the time goes in v5:
time: 73.1 us; the launch traced here: 72.3 us
  Pallas kernels  70.4 us (96%)
  local copies, waits for them, and re-layouts  1.24 us (2%)
    pallas_call x1, Pallas kernels, shards(): pl.pallas_call(body, name='cycle', out_shape=(jax.ShapeDtypeStruct((local...  70.4 us

profile of v5, /device:TPU:1, one launch (start us, length us, event | category | flops | bytes accessed | tf_op | source)
XLA Modules:
  0.0 72.3 jit_solution(6371838956416076959)
XLA Ops:
  0.6 70.4 %cycle.1 = (f32[12,16,128]{2,1,0:T(8,128)S(1)}, f32[8,192]{1,0:T(8,128)S(1)}) custom-call(f32[12,16,128]{2,1,0:T(8,128)} %refs_0_.1, f32[12,16,128]{2,1,0:T(8,128)} %refs_1_.1, f32[16,128]{1,0:T(8,128)} %refs_2_.1, s32[16,128]{1,0:T(8,128)} %refs_3_.1, s32[2,4096]{1,0:T(2,128)} %refs_4_.1, s32[1,1024]{1,0:T(1,128)} %bitcast.3, f32[1,1024]{1,0:T(1,128)} %bitcast.4, ...), custom_call_target="tpu_custom_call" | custom-call | tf_op jit(solution)/shard_map/cycle/pallas_call | solution.py:555
  71.0 0.6 copy.12
  71.7 0.6 copy.13

commit v6 on v5

--- a/solution.py
+++ b/solution.py
@@ -159,9 +159,9 @@
     head_ref, cond_ref, well_ref, lay_ref, pc_ref, oi_ref, ov_ref, os_ref = staged
     ret_ref, own_ref = refs[8:10]
     hx, cx, wx, fore, w_ref, h2_ref, vh_ref, khi, klo, ohi, olo, place, where = refs[10:23]
-    pcs, po, ro, mine, ao, flat, part, rs, turned, got, gpart, gred, gall, pile, snd, back = refs[23:39]
-    halo_s, halo_r, out_s, out_r, ro_s, ro_r, ao_s, ao_r = refs[39:47]
-    g1_s, g1_r, rs_s, rs_r, g2_s, g2_r, tu_s, tu_r, rt_s, rt_r = refs[47:]
+    pcs, wo_ref, po, ro, mine, ao, flat, part, rs, turned, got, gpart, gred, gall, pile, snd, back = refs[23:40]
+    halo_s, halo_r, out_s, out_r, ro_s, ro_r, ao_s, ao_r = refs[40:48]
+    g1_s, g1_r, rs_s, rs_r, g2_s, g2_r, tu_s, tu_r, rt_s, rt_r = refs[48:]
 
     slab, member = lax.axis_index("slab"), lax.axis_index("member")
     slabs, groups = lax.axis_size("slab"), lax.axis_size("member")
@@ -187,21 +187,21 @@
         lax.fori_loop(1, n, step, 0)
 
     def far_first(axis, body):
-        inner = groups // DEEP if axis == "member" else slabs // DEEP
+        if axis == "member":
+            inner = groups // DEEP
+            across = [lax.rem(member // DEEP + i, inner) * DEEP for i in range(inner)]
+            along = [lax.rem(member + i, DEEP) for i in range(DEEP)]
+            cores = [0]
+        else:
+            inner = slabs // (2 * DEEP)
+            across = [lax.rem(slab // (2 * DEEP) + i, inner) * (2 * DEEP) for i in range(inner)]
+            along = [lax.rem(slab // 2 + i, DEEP) * 2 for i in range(DEEP)]
+            cores = [lax.rem(slab, 2), lax.rem(slab + 1, 2)]
         for dz in (2, 1, 3, 0):
-
-            def step(i, carry):
-                if axis == "member":
-                    to = lax.rem(member // DEEP + i, inner) * DEEP
-                    to = to + lax.rem(member + dz, DEEP)
-                else:
-                    wide = 2 * DEEP
-                    to = lax.rem(slab // wide + i // 2, slabs // wide) * wide
-                    to = to + lax.rem(slab // 2 + dz, DEEP) * 2 + lax.rem(slab + i, 2)
-                body(to)
-                return carry
-
-            lax.fori_loop(1 if dz == 0 else 0, inner, step, 0)
+            for i in range(inner):
+                for c, core in enumerate(cores):
+                    if dz or i or c:
+                        body(across[i] + along[dz] + core)
 
     def copy(src, dst, ssem, rsem, axis, to):
         return pltpu.make_async_remote_copy(
@@ -224,8 +224,8 @@
         def start(self):
             far_first(self.axis, self.one)
 
-        def every(self):
-            part = self.dst.at[pl.ds(0, self.dst.shape[0] - 1)]
+        def every(self, n=None):
+            part = self.dst.at[pl.ds(0, n or self.dst.shape[0] - 1)]
             return copy(part, part, self.ssem, self.rsem, self.axis, other(1, self.axis))
 
         def arrive(self):
@@ -233,6 +233,9 @@
 
         def drain(self):
             self.every().wait_send()
+
+    height = gpart.shape[1]
+    owners = (members + 16 + height - 1) // height
 
     def total_of(ref):
         value = ref[0]
@@ -373,21 +376,20 @@
         w_ref[0:local, cols * i : cols * i + cols] = high
         w_ref[16 : 16 + local, cols * i : cols * i + cols] = low
 
-    def product(high_ref, low_ref, b):
-        total = jnp.dot(w_ref[...], high_ref[b], preferred_element_type=F32)
-        return total + jnp.dot(w_ref[...], low_ref[b], preferred_element_type=F32)
-
     shares = LANES // width
     each = local // shares
-    line = lax.broadcasted_iota(jnp.int32, (32, 32), 0)
-    col = lax.broadcasted_iota(jnp.int32, (32, 32), 1)
-    wanted = (line // 8) * each + lax.rem(line, 8)
+    line = lax.broadcasted_iota(jnp.int32, (64, 32), 0)
+    col = lax.broadcasted_iota(jnp.int32, (64, 32), 1)
+    wanted = lax.rem(line // 8, 4) * each + lax.rem(line, 8) + (line // 32) * 16
     valid = lax.rem(line, 8) < each
-    gather = jnp.where(valid & ((col == wanted) | (col == wanted + 16)), 1.0, 0.0)
+    gather = jnp.where(valid & (col == wanted), 1.0, 0.0).astype(BF16)
+    wo_ref[...] = jnp.dot(gather, w_ref[...], preferred_element_type=F32).astype(BF16)
     lane = lax.broadcasted_iota(jnp.int32, (8, LANES), 1) // width
     for n in range(obs_blocks):
         b = lax.rem(n + slab // (slabs // obs_blocks), obs_blocks)
-        total = mm(gather, product(ohi, olo, b))
+        total = jnp.dot(wo_ref[...], ohi[b], preferred_element_type=F32)
+        total += jnp.dot(wo_ref[...], olo[b], preferred_element_type=F32)
+        total = total[0:32] + total[32:64]
         for half in range(BLOCK // LANES):
             block = total[:, LANES * half : LANES * half + LANES]
             for u in range(shares):
@@ -413,7 +415,8 @@
 
     def whole(n, carry):
         b = lax.rem(n + slab // 2, blocks)
-        total = product(khi, klo, b)
+        total = jnp.dot(w_ref[...], khi[b], preferred_element_type=F32)
+        total += jnp.dot(w_ref[...], klo[b], preferred_element_type=F32)
         total = total[0:16] + total[16:32]
         for half in range(BLOCK // LANES):
             part[b * (BLOCK // LANES) + half] = total[0:local, LANES * half : LANES * half + LANES]
@@ -439,7 +442,6 @@
     send_mine.start()
     lax.fori_loop(LATE, blocks, every, 0)
     lax.fori_loop(FIRST, blocks, whole, 0)
-    lax.fori_loop(burst, slabs, send_parts, 0)
     send_obs.drain()
     send_mine.arrive()
     lane = lax.broadcasted_iota(jnp.int32, (4, LANES), 1)
@@ -459,17 +461,28 @@
     top = jnp.concatenate([gram[0:size, 0:size], gram[2 * size :, 2 * size :]], axis=1)
     pieces = [top, gram[size:, 0 : 2 * size], rhs[:, 0:LANES]]
     pieces.append(jnp.concatenate([rhs[:, LANES:], jnp.zeros((8, 2 * LANES - members), F32)], axis=1))
-    height = gpart.shape[1]
     pieces.append(jnp.zeros((slabs * height - members - 16, LANES), F32))
     gpart[...] = jnp.concatenate(pieces, axis=0).reshape(slabs, height, LANES)
-    send_gram.start()
+    far_first("slab", lambda to: pl.when(to < owners)(lambda: send_gram.one(to)))
+    lax.fori_loop(burst, slabs, send_parts, 0)
     rs[slab] = part[slab]
-    gred[slab] = gpart[slab]
     send_mine.drain()
-    send_gram.arrive()
-    gall[slab] = total_of(gred)
-    send_sum.start()
-    send_gram.drain()
+
+    @pl.when(slab < owners)
+    def _():
+        gred[slab] = gpart[slab]
+        send_gram.arrive()
+        gall[slab] = total_of(gred)
+        send_sum.start()
+
+    def owned(wait):
+        if owners == slabs:
+            wait(owners - 1)
+        else:
+            pl.when(slab < owners)(lambda: wait(owners - 1))
+            pl.when(slab >= owners)(lambda: wait(owners))
+
+    owned(lambda n: send_gram.every(n).wait_send())
     send_fore.arrive()
     pile[member] = fore[member]
     for n in range(groups):
@@ -480,7 +493,7 @@
     send_part.arrive()
     total = jnp.concatenate([total_of(rs), jnp.zeros((LANES - local, LANES), F32)], axis=0)
     turned[...] = total.T.reshape(groups, own, LANES)
-    send_sum.arrive()
+    owned(lambda n: send_sum.every(n).wait_recv())
     send_own.start()
     got[member] = turned[member]
     packed = gall[...].reshape(slabs * height, LANES)
@@ -503,7 +516,7 @@
         item.wait_send()
     send_fore.drain()
     send_part.drain()
-    send_sum.drain()
+    pl.when(slab < owners)(send_sum.drain)
     send_own.drain()
     send_back.arrive()
     for i in range(rows):
@@ -576,6 +589,7 @@
             f32(2 * pixels // LANES, LANES),
             f32(8, observed),
             f32(2, pixels),
+            bf16(64, rows * cols),
             f32(slabs, 4, LANES),
             f32(slabs, 4, LANES),
             f32(4, LANES),

time: 73.1 us -> 71.9 us (0.984)
  no operation moved by 1% of the time
where the time goes in v6:
time: 71.9 us; the launch traced here: 71.7 us
  Pallas kernels  69.8 us (97%)
  local copies, waits for them, and re-layouts  1.24 us (2%)
    pallas_call x1, Pallas kernels, shards(): pl.pallas_call(body, name='cycle', out_shape=(jax.ShapeDtypeStruct((local...  69.8 us

profile of v6, /device:TPU:1, one launch (start us, length us, event | category | flops | bytes accessed | tf_op | source)
XLA Modules:
  0.0 71.7 jit_solution(1611535713525273602)
XLA Ops:
  0.6 69.8 %cycle.1 = (f32[12,16,128]{2,1,0:T(8,128)S(1)}, f32[8,192]{1,0:T(8,128)S(1)}) custom-call(f32[12,16,128]{2,1,0:T(8,128)} %refs_0_.1, f32[12,16,128]{2,1,0:T(8,128)} %refs_1_.1, f32[16,128]{1,0:T(8,128)} %refs_2_.1, s32[16,128]{1,0:T(8,128)} %refs_3_.1, s32[2,4096]{1,0:T(2,128)} %refs_4_.1, s32[1,1024]{1,0:T(1,128)} %bitcast.3, f32[1,1024]{1,0:T(1,128)} %bitcast.4, ...), custom_call_target="tpu_custom_call" | custom-call | tf_op jit(solution)/shard_map/cycle/pallas_call | solution.py:568
  70.5 0.6 copy.12
  71.1 0.6 copy.13

commit v7 on v6

--- a/solution.py
+++ b/solution.py
@@ -39,10 +39,6 @@
 
 def mm(a, b):
     return dot(a, b, ((1,), (0,)))
-
-
-def mm_tn(a, b):
-    return dot(a, b, ((0,), (0,)))
 
 
 def mm_nt(a, b):
@@ -109,15 +105,18 @@
     gram = packed + jnp.where(row == col, members - 1.0, 0.0)
     corner = packed[0:size, size:] + jnp.where(row == col, members - 1.0, 0.0)[0:size, 0:size]
     l0 = inverse_factor(gram[0:size, 0:size])
-    t0 = mm_nt(l0, gram[size:, 0:size])
-    s1 = gram[size:, size:] - mm_tn(t0, t0[:, 0:size])
-    z1 = -mm_tn(t0, l0)
-    l1 = inverse_factor(s1[0:size])
-    t1 = mm_nt(l1, s1[size:])
-    l10 = mm(l1, z1[0:size])
-    s2 = corner - mm_tn(t0[:, size:], t0[:, size:]) - mm_tn(t1, t1)
-    z2 = jnp.concatenate([z1[size:] - mm_tn(t1, l10), -mm_tn(t1, l1)], axis=1)
-    l2 = inverse_factor(s2)
+    f10 = mm_nt(gram[size : 2 * size, 0:size], l0)
+    s11 = gram[size : 2 * size, size:] - mm_nt(f10, f10)
+    f20 = mm_nt(gram[2 * size :, 0:size], l0)
+    s21 = gram[2 * size :, size:] - mm_nt(f20, f10)
+    s22 = corner - mm_nt(f20, f20)
+    z10 = mm(f10, l0)
+    z20 = mm(f20, l0)
+    l1 = inverse_factor(s11)
+    f21 = mm_nt(s21, l1)
+    l10 = -mm(l1, z10)
+    l2 = inverse_factor(s22 - mm_nt(f21, f21))
+    z2 = jnp.concatenate([-(z20 + mm(f21, l10)), -mm(f21, l1)], axis=1)
     l20 = mm(l2, z2)
     zero = jnp.zeros((size, size), F32)
     inverse = jnp.concatenate(
@@ -385,11 +384,18 @@
     gather = jnp.where(valid & (col == wanted), 1.0, 0.0).astype(BF16)
     wo_ref[...] = jnp.dot(gather, w_ref[...], preferred_element_type=F32).astype(BF16)
     lane = lax.broadcasted_iota(jnp.int32, (8, LANES), 1) // width
-    for n in range(obs_blocks):
-        b = lax.rem(n + slab // (slabs // obs_blocks), obs_blocks)
+    order = [lax.rem(n + slab // (slabs // obs_blocks), obs_blocks) for n in range(obs_blocks)]
+
+    def seen(b):
         total = jnp.dot(wo_ref[...], ohi[b], preferred_element_type=F32)
         total += jnp.dot(wo_ref[...], olo[b], preferred_element_type=F32)
-        total = total[0:32] + total[32:64]
+        return total[0:32] + total[32:64]
+
+    ahead = seen(order[0])
+    for n, b in enumerate(order):
+        total = ahead
+        if n + 1 < obs_blocks:
+            ahead = seen(order[n + 1])
         for half in range(BLOCK // LANES):
             block = total[:, LANES * half : LANES * half + LANES]
             for u in range(shares):
@@ -400,7 +406,7 @@
                 po[(b * (BLOCK // LANES) + half) * shares + u] = chunk[0:4]
         count = slabs // obs_blocks
 
-        def send(i, carry):
+        def send(i, carry, b=b):
             to = b * count + lax.rem(i + slab, count)
 
             @pl.when(to != slab)

time: 71.9 us -> 70.9 us (0.986)
  Pallas kernels: 69.8 us -> 68.2 us
    pallas_call x1, Pallas kernels: 69.8 us -> 68.2 us  [shards(): pl.pallas_call(body, name='cycle', out_shape=(jax.ShapeDtypeStruct((local...]
where the time goes in v7:
time: 70.9 us; the launch traced here: 70 us
  Pallas kernels  68.2 us (96%)
  local copies, waits for them, and re-layouts  1.24 us (2%)
    pallas_call x1, Pallas kernels, shards(): pl.pallas_call(body, name='cycle', out_shape=(jax.ShapeDtypeStruct((local...  68.2 us

profile of v7, /device:TPU:1, one launch (start us, length us, event | category | flops | bytes accessed | tf_op | source)
XLA Modules:
  0.0 70.0 jit_solution(11727500237645308010)
XLA Ops:
  0.6 68.2 %cycle.1 = (f32[12,16,128]{2,1,0:T(8,128)S(1)}, f32[8,192]{1,0:T(8,128)S(1)}) custom-call(f32[12,16,128]{2,1,0:T(8,128)} %refs_0_.1, f32[12,16,128]{2,1,0:T(8,128)} %refs_1_.1, f32[16,128]{1,0:T(8,128)} %refs_2_.1, s32[16,128]{1,0:T(8,128)} %refs_3_.1, s32[2,4096]{1,0:T(2,128)} %refs_4_.1, s32[1,1024]{1,0:T(1,128)} %bitcast.3, f32[1,1024]{1,0:T(1,128)} %bitcast.4, ...), custom_call_target="tpu_custom_call" | custom-call | tf_op jit(solution)/shard_map/cycle/pallas_call | solution.py:574
  68.8 0.6 copy.12
  69.4 0.6 copy.13

commit v8 on v7

--- a/solution.py
+++ b/solution.py
@@ -18,9 +18,10 @@
 BLOCK = 256
 LANES = 128
 EARLY = 3
-MIDDLE = 9
-LATE = 11
+MIDDLE = 8
+LATE = 10
 FIRST = 7
+SECOND = 14
 DEEP = 4
 
 
@@ -447,7 +448,7 @@
     ao[member] = total
     send_mine.start()
     lax.fori_loop(LATE, blocks, every, 0)
-    lax.fori_loop(FIRST, blocks, whole, 0)
+    lax.fori_loop(FIRST, SECOND, whole, 0)
     send_obs.drain()
     send_mine.arrive()
     lane = lax.broadcasted_iota(jnp.int32, (4, LANES), 1)
@@ -470,6 +471,7 @@
     pieces.append(jnp.zeros((slabs * height - members - 16, LANES), F32))
     gpart[...] = jnp.concatenate(pieces, axis=0).reshape(slabs, height, LANES)
     far_first("slab", lambda to: pl.when(to < owners)(lambda: send_gram.one(to)))
+    lax.fori_loop(SECOND, blocks, whole, 0)
     lax.fori_loop(burst, slabs, send_parts, 0)
     rs[slab] = part[slab]
     send_mine.drain()

time: 70.9 us -> 71.2 us (level)
  no operation moved by 1% of the time
where the time goes in v8:
time: 71.2 us; the launch traced here: 70.3 us
  Pallas kernels  68.4 us (96%)
  local copies, waits for them, and re-layouts  1.24 us (2%)
    pallas_call x1, Pallas kernels, shards(): pl.pallas_call(body, name='cycle', out_shape=(jax.ShapeDtypeStruct((local...  68.4 us

profile of v8, /device:TPU:1, one launch (start us, length us, event | category | flops | bytes accessed | tf_op | source)
XLA Modules:
  0.0 70.3 jit_solution(15771891553410012839)
XLA Ops:
  0.6 68.4 %cycle.1 = (f32[12,16,128]{2,1,0:T(8,128)S(1)}, f32[8,192]{1,0:T(8,128)S(1)}) custom-call(f32[12,16,128]{2,1,0:T(8,128)} %refs_0_.1, f32[12,16,128]{2,1,0:T(8,128)} %refs_1_.1, f32[16,128]{1,0:T(8,128)} %refs_2_.1, s32[16,128]{1,0:T(8,128)} %refs_3_.1, s32[2,4096]{1,0:T(2,128)} %refs_4_.1, s32[1,1024]{1,0:T(1,128)} %bitcast.3, f32[1,1024]{1,0:T(1,128)} %bitcast.4, ...), custom_call_target="tpu_custom_call" | custom-call | tf_op jit(solution)/shard_map/cycle/pallas_call | solution.py:576
  69.1 0.6 copy.12
  69.7 0.6 copy.13
